TPU v7x, 32 devices: a whole 2x2x4 slice. The times are simulated.
32 devices in a mesh: tok: 8 (over z, x), mdl: 4 (over y, core).
Axes of the slice: x: 2, y: 2, z: 4, core: 2. Of those that a mesh axis runs over, the one named last changes fastest.
Arguments:
- tokens: bfloat16 [10240, 1152], P('tok', 'mdl'), may hold values from -6 to 6
- cotangent: bfloat16 [10240, 1152], P('tok', 'mdl'), may hold values from -6 to 6
- lengths: int32 [8, 6], P('tok'), may hold values from 0 to 512, as said below
- padding: int32 [8, 6], P('tok'), may hold values from 0 to 63, as said below
- timesteps: int32 [8, 6], P('tok'), may hold values from 0 to 999
- labels: int32 [8, 6], P('tok'), may hold values from 0 to 999
- head_mask: int32 [8, 6, 16], P('tok', None, 'mdl'), may hold values 0 or 1
- chan_mask: int32 [8, 6, 16], P('tok', None, 'mdl'), may hold values 0 or 1
- keep_mask: int32 [10240], P('tok'), may hold values 0 or 1
- qkv_weight: bfloat16 [1152, 3, 1152], P('tok', None, 'mdl'), may hold values from -0.1875 to 0.1875
- qv_bias: bfloat16 [2, 1152], P(None, 'mdl'), may hold values from -3 to 3
- out_weight: bfloat16 [1152, 1152], P('mdl', 'tok'), may hold values from -0.375 to 0.375
- out_bias: bfloat16 [1152], P('mdl'), may hold values from -2 to 2
- up_weight: bfloat16 [1152, 4608], P('tok', 'mdl')
- up_bias: bfloat16 [4608], P('mdl'), may hold values from -3 to 3
- down_weight: bfloat16 [4608, 1152], P('mdl', 'tok'), may hold values from -0.125 to 0.125
- down_bias: bfloat16 [1152], P('mdl'), may hold values from -3 to 3
- ada_weight: bfloat16 [1152, 6, 1152], P('tok', None, 'mdl'), may hold values from -0.1875 to 0.1875
- ada_bias: bfloat16 [6, 1152], P(None, 'mdl'), may hold values from -3 to 3
- time_weight: bfloat16 [256, 1152], P('tok', 'mdl'), may hold values from -0.375 to 0.375
- class_table: bfloat16 [1000, 1152], P(None, 'mdl'), may hold values from -5 to 5
Outputs:
- output: bfloat16 [10240, 1152], P('tok', 'mdl')
- grad_tokens: float32 [10240, 1152], P('tok', 'mdl')
- grad_qkv_weight: float32 [1152, 3, 1152], P('tok', None, 'mdl')
- grad_qv_bias: float32 [2, 1152], P(None, 'mdl')
- grad_out_weight: float32 [1152, 1152], P('mdl', 'tok')
- grad_out_bias: float32 [1152], P('mdl')
- grad_up_weight: float32 [1152, 4608], P('tok', 'mdl')
- grad_up_bias: float32 [4608], P('mdl')
- grad_down_weight: float32 [4608, 1152], P('mdl', 'tok')
- grad_down_bias: float32 [1152], P('mdl')
- grad_ada_weight: float32 [1152, 6, 1152], P('tok', None, 'mdl')
- grad_ada_bias: float32 [6, 1152], P(None, 'mdl')
- grad_time_weight: float32 [256, 1152], P('tok', 'mdl')
- grad_class_table: float32 [1000, 1152], P(None, 'mdl')
Inputs may be any that keep to these rules, and one draw needn't show every extreme that they name: `lengths`: slot 0 of every row holds a crop; a slot's length is 0 (no crop) or 128 to 512. padding[r, j] tokens of padding follow crop slot j; the lengths and padding of a row sum to at most 1280, and the rest of the row is padding as well.
All inputs are finite; a program needn't handle non-finite values. No bound on the sum of `head_mask` or of `chan_mask` or of `keep_mask` on one device may be relied on, other than what follows from the above.
Results may differ from a plain program's by a relative error of at most 0.029.
The roundings to bfloat16 on the way count: a program that leaves them out, or rounds other values in their place, can miss the bound.
Values may be sent and summed in bfloat16 or wider, within the bound.
A program may use at most 192 MiB of HBM per device.

v0:
```python
import math

import jax
import jax.numpy as jnp
from jax import lax
from jax.experimental import pallas as pl
from jax.experimental.pallas import tpu as pltpu
from jax.sharding import PartitionSpec as P

norm_floor = 1e-06
unseen = -1e30
f32 = jnp.float32
bf16 = jnp.bfloat16


def exact_dot(left, right):
    return jnp.dot(left, right, precision=lax.Precision.HIGHEST, preferred_element_type=f32)


def mm(left, right, dims):
    return lax.dot_general(left, right, (dims, ((), ())), preferred_element_type=f32)


def timestep_features(steps, freq_count):
    half_freq = freq_count // 2
    freq_rates = jnp.exp(-math.log(10000.0) * jnp.arange(half_freq, dtype=f32) / half_freq)
    angles = steps.astype(f32)[:, None] * freq_rates[None, :]
    return jnp.concatenate([jnp.cos(angles), jnp.sin(angles)], axis=1)


def crop_layout(lengths, padding, row_len):
    span_sums = lengths + padding
    starts = jnp.cumsum(span_sums, axis=1) - span_sums
    positions = jnp.arange(row_len, dtype=jnp.int32)
    inside = (positions[None, :, None] >= starts[:, None, :]) & (
        positions[None, :, None] < (starts + lengths)[:, None, :]
    )
    slot_ids = jnp.arange(lengths.shape[1], dtype=jnp.int32)
    segment = jnp.min(jnp.where(inside, slot_ids[None, None, :], lengths.shape[1]), axis=2)
    return (inside, segment)


def norm_rows(values):
    row_mean = jnp.mean(values, axis=1, keepdims=True)
    row_var = jnp.mean(values * values, axis=1, keepdims=True) - row_mean * row_mean
    inverse = lax.rsqrt(row_var + norm_floor)
    return ((values - row_mean) * inverse, inverse)


def gather_cols(rows_low):
    return lax.all_gather(rows_low, "mdl", axis=1, tiled=True)


def scatter_cols(partial_rows):
    return lax.psum_scatter(partial_rows.astype(bf16), "mdl", scatter_dimension=1, tiled=True)


def attend_row(queries, key_rows, value_rows, segment, score_scale):
    raw_scores = jnp.einsum("qhd,khd->hqk", queries, key_rows, preferred_element_type=f32) * score_scale
    same_crop = segment[:, None] == segment[None, :]
    raw_scores = jnp.where(same_crop[None], raw_scores, unseen)
    row_max = jnp.max(raw_scores, axis=2, keepdims=True)
    expo_terms = jnp.exp(raw_scores - row_max)
    row_total = jnp.sum(expo_terms, axis=2, keepdims=True)
    prob_low = (expo_terms / row_total).astype(bf16)
    attend = jnp.einsum("hqk,khd->qhd", prob_low, value_rows, preferred_element_type=f32)
    return (attend, (row_max + jnp.log(row_total))[:, :, 0])


def attend_back(queries, key_rows, value_rows, segment, logsum_rows, grad_att, score_scale):
    raw_scores = jnp.einsum("qhd,khd->hqk", queries, key_rows, preferred_element_type=f32) * score_scale
    same_crop = segment[:, None] == segment[None, :]
    raw_scores = jnp.where(same_crop[None], raw_scores, unseen)
    prob_full = jnp.exp(raw_scores - logsum_rows[:, :, None])
    grad_prob = jnp.einsum("qhd,khd->hqk", grad_att, value_rows, preferred_element_type=f32)
    inner_sum = jnp.sum(prob_full * grad_prob, axis=2, keepdims=True)
    grad_scores = (prob_full * (grad_prob - inner_sum)).astype(bf16)
    grad_queries = jnp.einsum("hqk,khd->qhd", grad_scores, key_rows, preferred_element_type=f32) * score_scale
    grad_keys = jnp.einsum("hqk,qhd->khd", grad_scores, queries, preferred_element_type=f32) * score_scale
    grad_values = jnp.einsum("hqk,qhd->khd", prob_full.astype(bf16), grad_att, preferred_element_type=f32)
    return (grad_queries, grad_keys, grad_values)


def peer(tok=None, mdl=None):
    where = {}
    if tok is not None:
        where["tok"] = tok
    if mdl is not None:
        where["mdl"] = mdl
    return where


def remote(src, dst, send_sem, recv_sem, where):
    return pltpu.make_async_remote_copy(
        src_ref=src, dst_ref=dst, send_sem=send_sem, recv_sem=recv_sem, device_id=where, device_id_type=pl.DeviceIdType.MESH
    )


def greet(tok_at, mdl_at, tok_count, mdl_count):
    barrier = pltpu.get_barrier_semaphore()
    for step in range(1, tok_count):
        pl.semaphore_signal(
            barrier, inc=1, device_id=peer(tok=lax.rem(tok_at + step, tok_count)), device_id_type=pl.DeviceIdType.MESH
        )
    for step in range(1, mdl_count):
        pl.semaphore_signal(
            barrier, inc=1, device_id=peer(mdl=lax.rem(mdl_at + step, mdl_count)), device_id_type=pl.DeviceIdType.MESH
        )
    pl.semaphore_wait(barrier, tok_count + mdl_count - 2)


def split_two(values):
    high = values.astype(bf16)
    return high, (values - high.astype(f32)).astype(bf16)


def split_three(values):
    high, rest = split_two(values)
    return high, rest, (values - high.astype(f32) - rest.astype(f32)).astype(bf16)


class AllToPeers:
    def __init__(self, axis, me, count, send_sems, recv_sems):
        self.axis, self.me, self.count, self.send_sems, self.recv_sems = axis, me, count, send_sems, recv_sems

    def copies(self, source, slots):
        for step in range(1, self.count):
            other = lax.rem(self.me + step, self.count)
            yield remote(
                source(other), slots.at[self.me], self.send_sems.at[step], self.recv_sems.at[self.me], peer(**{self.axis: other})
            )

    def start(self, source, slots):
        for copy in self.copies(source, slots):
            copy.start()

    def wait_recv(self, source, slots):
        for step in range(1, self.count):
            other = lax.rem(self.me + step, self.count)
            remote(
                source(other), slots.at[other], self.send_sems.at[step], self.recv_sems.at[other], peer(**{self.axis: other})
            ).wait_recv()

    def wait_send(self, source, slots):
        for copy in self.copies(source, slots):
            copy.wait_send()


class LineGather:
    def __init__(self, tok_at, shard, full, columns, rows, sends, recv_sems):
        self.tok_at, self.full, self.columns, self.rows = tok_at, full, columns, rows
        self.shard = shard.at[:, columns]
        self.sems = [sends.at[kind] for kind in range(3)]
        self.recv_sems = recv_sems
        self.line = lax.div(tok_at, 2)
        self.side = lax.rem(tok_at, 2)
        self.across = tok_at + 1 - 2 * self.side

    def slot(self, owner):
        return self.full.at[pl.ds(pl.multiple_of(owner * self.rows, 16), self.rows), self.columns]

    def copy(self, kind, owner, own=False):
        target = (self.tok_at + 2, self.tok_at - 2, self.across)[kind]
        source = self.shard if own else self.slot(owner)
        return remote(source, self.slot(owner), self.sems[kind].at[owner], self.recv_sems.at[owner], peer(tok=target))

    def each_send(self, step, act):
        if step == 0:
            pl.when(self.line < 3)(lambda: act(self.copy(0, self.tok_at, True)))
            pl.when(self.line > 0)(lambda: act(self.copy(1, self.tok_at, True)))
            act(self.copy(2, self.tok_at, True))
        else:
            below = self.tok_at - 2 * step
            above = self.tok_at + 2 * step
            pl.when((self.line >= step) & (self.line < 3))(lambda: act(self.copy(0, below)))
            pl.when((self.line + step <= 3) & (self.line > 0))(lambda: act(self.copy(1, above)))
            pl.when(self.line >= step)(lambda: act(self.copy(2, below)))
            pl.when(self.line + step <= 3)(lambda: act(self.copy(2, above)))

    def start(self):
        self.each_send(0, lambda copy: copy.start())

    def arrive(self, owner):
        self.copy(2, owner).wait_recv()

    def forward(self, step):
        pl.when(self.line >= step)(lambda: self.arrive(self.tok_at - 2 * step))
        pl.when(self.line + step <= 3)(lambda: self.arrive(self.tok_at + 2 * step))
        self.each_send(step, lambda copy: copy.start())

    def arrive_across(self):
        for place in range(4):
            self.arrive(2 * place + 1 - self.side)

    def wait_send(self):
        for step in range(4):
            self.each_send(step, lambda copy: copy.wait_send())


class QuadGather:
    def __init__(self, mdl_at, own, blocks, chunks, chunk_rows, far_sems, near_sems, hand_sems, recv_sems):
        self.mdl_at, self.own, self.blocks, self.chunks, self.chunk_rows = mdl_at, own, blocks, chunks, chunk_rows
        self.far_sems, self.near_sems, self.hand_sems, self.recv_sems = far_sems, near_sems, hand_sems, recv_sems
        self.far = lax.rem(mdl_at + 2, 4)
        self.near = mdl_at + 1 - 2 * lax.rem(mdl_at, 2)
        self.far_near = lax.rem(self.near + 2, 4)

    def place(self, owner, chunk):
        return self.blocks.at[owner, pl.ds(chunk * self.chunk_rows, self.chunk_rows), :]

    def far_copy(self, chunk):
        source = self.own.at[pl.ds(chunk * self.chunk_rows, self.chunk_rows), :]
        return remote(
            source, self.place(self.mdl_at, chunk), self.far_sems.at[chunk], self.recv_sems.at[self.mdl_at, chunk], peer(mdl=self.far)
        )

    def near_copy(self, chunk):
        source = self.own.at[pl.ds(chunk * self.chunk_rows, self.chunk_rows), :]
        return remote(
            source, self.place(self.mdl_at, chunk), self.near_sems.at[chunk], self.recv_sems.at[self.mdl_at, chunk], peer(mdl=self.near)
        )

    def hand_copy(self, chunk):
        return remote(
            self.place(self.far, chunk),
            self.place(self.far, chunk),
            self.hand_sems.at[chunk],
            self.recv_sems.at[self.far, chunk],
            peer(mdl=self.near),
        )

    def arrive(self, owner, chunk):
        remote(
            self.place(owner, chunk), self.place(owner, chunk), self.hand_sems.at[chunk], self.recv_sems.at[owner, chunk], peer(mdl=self.near)
        ).wait_recv()

    def start(self, chunks):
        for chunk in chunks:
            self.far_copy(chunk).start()
        for chunk in chunks:
            self.near_copy(chunk).start()

    def hand(self, chunk):
        self.arrive(self.far, chunk)
        self.hand_copy(chunk).start()

    def arrive_rest(self, chunk):
        self.arrive(self.near, chunk)
        self.arrive(self.far_near, chunk)

    def wait_send(self):
        for chunk in range(self.chunks):
            self.far_copy(chunk).wait_send()
            self.near_copy(chunk).wait_send()
            self.hand_copy(chunk).wait_send()


class RowReduce:
    def __init__(self, mdl_at, part, near_in, own_sum, far_in, full, sends, recvs):
        self.part, self.near_in, self.own_sum, self.far_in, self.full = part, near_in, own_sum, far_in, full
        self.sends, self.recvs = sends, recvs
        self.core = lax.rem(mdl_at, 2)
        self.far = peer(mdl=lax.rem(mdl_at + 2, 4))
        self.near = peer(mdl=mdl_at + 1 - 2 * self.core)
        self.half = near_in.shape[1]

    def rows(self, chunk, core):
        return pl.ds(pl.multiple_of((2 * chunk + core) * self.half, 128), self.half)

    def near_copy(self, chunk):
        source = self.part.at[self.rows(chunk, 1 - self.core), :]
        return remote(source, self.near_in.at[chunk], self.sends.at[0, chunk], self.recvs.at[0, chunk], self.near)

    def far_copy(self, chunk):
        return remote(self.own_sum.at[chunk], self.far_in.at[chunk], self.sends.at[1, chunk], self.recvs.at[1, chunk], self.far)

    def share_copy(self, chunk):
        place = self.full.at[self.rows(chunk, self.core), :]
        return remote(place, place, self.sends.at[2, chunk], self.recvs.at[2, chunk], self.near)

    def first(self, chunk):
        self.near_copy(chunk).start()

    def second(self, chunk):
        self.near_copy(chunk).wait_recv()
        own = self.part[self.rows(chunk, self.core), :].astype(f32)
        self.own_sum[chunk] = (own + self.near_in[chunk].astype(f32)).astype(bf16)
        self.far_copy(chunk).start()

    def third(self, chunk):
        self.far_copy(chunk).wait_recv()
        total = self.own_sum[chunk].astype(f32) + self.far_in[chunk].astype(f32)
        self.full[self.rows(chunk, self.core), :] = total.astype(bf16)
        self.share_copy(chunk).start()

    def fourth(self, chunk):
        place = self.full.at[self.rows(chunk, 1 - self.core), :]
        remote(place, place, self.sends.at[2, chunk], self.recvs.at[2, chunk], self.near).wait_recv()

    def wait_send(self, chunk):
        self.near_copy(chunk).wait_send()
        self.far_copy(chunk).wait_send()
        self.share_copy(chunk).wait_send()


def greet_quad(mdl_at):
    barrier = pltpu.get_barrier_semaphore()
    for step in range(1, 4):
        pl.semaphore_signal(
            barrier, inc=1, device_id=peer(mdl=lax.rem(mdl_at + step, 4)), device_id_type=pl.DeviceIdType.MESH
        )
    pl.semaphore_wait(barrier, 3)


def centre(values):
    center = values - jnp.mean(values, axis=1, keepdims=True)
    inverse = lax.rsqrt(jnp.mean(center * center, axis=1, keepdims=True) + norm_floor)
    return center * inverse, inverse


def front_kernel(
    feats_own,
    class_flip,
    time_own,
    ada_parts,
    ada_bias,
    qv_bias,
    bias_table,
    qkv_parts,
    out_flip,
    up_own,
    down_flip,
    token_flip,
    cot_flip,
    lengths,
    padding,
    labels,
    masks,
    keep_table,
    small_all,
    embedding_out,
    cond_out,
    out_bias_full,
    pieces,
    own_pieces,
    hot,
    hot_keep,
    head_rows,
    chan_rows,
    seg_row,
    unit_full,
    cot_blocks,
    tokens_full,
    qkv_full,
    out_full,
    mod_one,
    stats,
    q_heads,
    k_heads,
    v_heads,
    logsum,
    attended,
    branch_full,
    tokens,
    cotangent,
    out_row,
    up_row,
    down_row,
    small_own,
    head_shard,
    unit_shard,
    head_full,
    token_blocks,
    time_all,
    cond_blocks,
    mod_parts,
    mod_slots,
    mod_out,
    late_parts,
    late_slots,
    late_out,
    mask_room,
    v_flip,
    att_heads,
    branch_part,
    near_in,
    own_sum,
    far_in,
    small_send,
    small_recv,
    time_send,
    time_recv,
    cond_send,
    cond_recv,
    part_send,
    part_recv,
    mod_send,
    mod_recv,
    late_part_send,
    late_part_recv,
    late_mod_send,
    late_mod_recv,
    line_sends,
    line_recvs,
    quad_sends,
    quad_recvs,
    sum_sends,
    sum_recvs,
    own_sems,
):
    tok_at = lax.axis_index("tok")
    mdl_at = lax.axis_index("mdl")
    tok_count, slots = small_all.shape[0], small_all.shape[1]
    freq_count = time_all.shape[0] * time_all.shape[1]
    local_width = time_own.shape[1]
    own_rows = head_shard.shape[0]
    heads, rows, head_width = q_heads.shape
    score_scale = 1.0 / math.sqrt(head_width)
    greet(tok_at, mdl_at, tok_count, 4)

    small = AllToPeers("tok", tok_at, tok_count, small_send, small_recv)
    times = AllToPeers("tok", tok_at, tok_count, time_send, time_recv)
    conds = AllToPeers("mdl", mdl_at, 4, cond_send, cond_recv)
    parts = AllToPeers("tok", tok_at, tok_count, part_send, part_recv)
    mods = AllToPeers("mdl", mdl_at, 4, mod_send, mod_recv)
    late_shares = AllToPeers("tok", tok_at, tok_count, late_part_send, late_part_recv)
    late_mods = AllToPeers("mdl", mdl_at, 4, late_mod_send, late_mod_recv)
    head_line = LineGather(
        tok_at, head_shard, head_full, pl.ds(0, head_shard.shape[1]), own_rows, line_sends.at[0], line_recvs.at[0]
    )
    unit_pieces = line_recvs.shape[0] - 1
    unit_piece = unit_shard.shape[1] // unit_pieces
    unit_lines = [
        LineGather(
            tok_at,
            unit_shard,
            unit_full,
            pl.ds(part * unit_piece, unit_piece),
            own_rows,
            line_sends.at[1 + part],
            line_recvs.at[1 + part],
        )
        for part in range(unit_pieces)
    ]
    unit_order = tuple((distance, part) for distance in range(1, 4) for part in range(unit_pieces))

    def forward_units(here, schedule):
        for at, index in schedule:
            distance, part = unit_order[index]
            pl.when(here == at)(lambda distance=distance, part=part: unit_lines[part].forward(distance))

    chunks = quad_recvs.shape[2]
    size = rows // chunks
    token_quad = QuadGather(
        mdl_at, tokens, token_blocks, chunks, size, quad_sends.at[0, 0], quad_sends.at[0, 1], quad_sends.at[0, 2], quad_recvs.at[0]
    )
    cot_quad = QuadGather(
        mdl_at, cotangent, cot_blocks, chunks, size, quad_sends.at[1, 0], quad_sends.at[1, 1], quad_sends.at[1, 2], quad_recvs.at[1]
    )
    branch = RowReduce(mdl_at, branch_part, near_in, own_sum, far_in, branch_full, sum_sends, sum_recvs)

    times.start(lambda other: time_own, time_all)
    slot_count = lengths.shape[1]
    class_count = class_flip.shape[1]
    label_at = lax.broadcasted_iota(jnp.int32, (slots, class_count), 0)
    class_at = lax.broadcasted_iota(jnp.int32, (slots, class_count), 1)
    chosen = jnp.zeros((slots, class_count), f32)
    label_rows = jnp.zeros((slots, small_own.shape[1] - freq_count - local_width), f32)
    label_row_at = lax.broadcasted_iota(jnp.int32, label_rows.shape, 0)
    for at in range(slot_count):
        chosen = jnp.where((label_at == at) & (class_at == labels[0, at]), 1.0, chosen)
        label_rows = jnp.where(label_row_at == at, labels[0, at].astype(f32), label_rows)
    small_own[...] = jnp.concatenate(
        [feats_own[...], mm(chosen.astype(bf16), class_flip[...], ((1,), (1,))), label_rows], axis=1
    )
    small.start(lambda other: small_own, small_all)
    head_shard[...] = jnp.concatenate([qkv_parts[0], qkv_parts[1], qkv_parts[2], out_flip[...]], axis=1)
    units = up_own.shape[1]
    unit_shard[:, :units] = up_own[...]
    unit_shard[:, units:] = down_flip[...]
    head_line.start()
    tokens[...] = token_flip[...].T
    cotangent[...] = cot_flip[...].T
    token_quad.start((0, 1))
    own_copies = (
        pltpu.make_async_copy(head_shard, head_line.slot(tok_at), own_sems.at[0]),
        pltpu.make_async_copy(
            unit_shard, unit_full.at[pl.ds(pl.multiple_of(tok_at * own_rows, 16), own_rows), :], own_sems.at[1]
        ),
        pltpu.make_async_copy(tokens, token_blocks.at[mdl_at], own_sems.at[2]),
        pltpu.make_async_copy(cotangent, cot_blocks.at[mdl_at], own_sems.at[3]),
    )
    for copy in own_copies:
        copy.start()
    small_all[tok_at] = small_own[...]
    time_all[tok_at] = time_own[...]

    def row_of(first, length):
        lanes = bias_table.shape[1]
        count = -(-length // lanes)
        return jnp.concatenate([bias_table[at : at + 1, :] for at in range(first, first + count)], axis=1)[:, :length]

    out_rows = -(-local_width // bias_table.shape[1])
    up_rows = units // bias_table.shape[1]
    out_bias_own = row_of(0, local_width)
    out_row[...] = out_bias_own
    up_row[...] = row_of(2 * out_rows, units)
    down_row[...] = row_of(out_rows, local_width)
    keep_row = jnp.concatenate([keep_table[at : at + 1, :] for at in range(keep_table.shape[0])], axis=1)

    positions = lax.broadcasted_iota(jnp.int32, (slots, rows), 1)
    slot_rows = lax.broadcasted_iota(jnp.int32, (slots, rows), 0)
    crop_rows = jnp.zeros((slots, rows), f32)
    segments = jnp.full((slots, rows), float(slot_count), f32)
    begin = jnp.int32(0)
    for at in range(slot_count):
        finish = begin + lengths[0, at]
        inside = (positions >= begin) & (positions < finish)
        crop_rows = jnp.where(inside & (slot_rows == at), 1.0, crop_rows)
        segments = jnp.where(inside & (segments == float(slot_count)), float(at), segments)
        begin = finish + padding[0, at]
    seg_row[...] = segments
    stats[:, 2:3] = segments.T[:, 0:1]
    triple = jnp.concatenate([crop_rows, crop_rows, crop_rows, jnp.zeros_like(crop_rows)], axis=0)
    hot[...] = triple.T.astype(bf16)
    hot_keep[...] = (triple * keep_row.astype(f32)).T.astype(bf16)
    mask_room[...] = jnp.zeros_like(mask_room)
    mask_room[:slot_count, : masks.shape[2]] = masks[0].astype(f32)
    groups_all = masks.shape[2]
    for from_at, groups, out in ((0, heads, head_rows), (heads, groups_all - heads, chan_rows)):
        wide = out.shape[1]
        group_at = lax.broadcasted_iota(jnp.int32, (slots, wide), 1)
        spread_mask = jnp.zeros((slots, wide), f32)
        for group in range(groups):
            first, last = group * (wide // groups), (group + 1) * (wide // groups)
            spread_mask = jnp.where((group_at >= first) & (group_at < last), mask_room[:, from_at + group : from_at + group + 1], spread_mask)
        out[...] = jnp.concatenate([spread_mask] + [jnp.zeros_like(spread_mask)] * 3, axis=0).astype(bf16)
    qv_rows = qv_bias[...].astype(f32)
    qkv_bias = jnp.concatenate([qv_rows[0:1], jnp.zeros((1, local_width), f32), qv_rows[1:2]], axis=1)

    small.wait_recv(lambda other: small_own, small_all)
    times.wait_recv(lambda other: time_own, time_all)

    feats = small_all[:, :, :freq_count].reshape(tok_count * slots, freq_count)
    time_full = time_all[...].reshape(freq_count, local_width)
    embedding = small_all[:, :, freq_count : freq_count + local_width].reshape(tok_count * slots, local_width)
    for piece in split_three(feats):
        embedding = embedding + mm(piece, time_full, ((1,), (0,)))
    embedding_out[...] = embedding
    cond_blocks[mdl_at] = (embedding / (1.0 + jnp.exp(-embedding))).astype(bf16)
    conds.start(lambda other: cond_blocks.at[mdl_at], cond_blocks)
    conds.wait_recv(lambda other: cond_blocks.at[mdl_at], cond_blocks)
    cond_block = cond_blocks[lax.div(tok_at, 2)].astype(f32)
    cond_own = jnp.where(lax.rem(tok_at, 2) == 0, cond_block[:, :own_rows], cond_block[:, own_rows:]).astype(bf16)
    cond_out[...] = cond_own
    mod_parts[...] = jnp.concatenate([mm(cond_own, ada_parts[part], ((1,), (0,))) for part in range(2)], axis=1).reshape(
        mod_parts.shape
    )
    parts.start(lambda other: mod_parts.at[other], mod_slots)
    head_line.forward(1)
    late_parts[...] = jnp.concatenate([mm(cond_own, ada_parts[part], ((1,), (0,))) for part in range(2, 6)], axis=1).reshape(
        late_parts.shape
    )
    bias_rows = ada_bias[...].astype(f32)
    slot_at = lax.broadcasted_iota(jnp.int32, (slots, local_width), 0)

    def add_bias(part, values):
        added = jnp.where(slot_at < slot_count, bias_rows[part : part + 1], 0.0)
        if part == 0:
            added = jnp.where(slot_at == slot_count, out_bias_own, added)
        return values + added

    def total_of(mine, parts_own, slots_in):
        slots_in[tok_at] = parts_own[tok_at]
        mine.wait_recv(lambda other: parts_own.at[other], slots_in)
        values = slots_in[0]
        for source in range(1, tok_count):
            values = values + slots_in[source]
        return values

    def place_pieces(first_part, ref):
        count = ref.shape[2] // local_width
        for at in range(count):
            part = first_part + at
            columns = slice(at * local_width, (at + 1) * local_width)
            joined = jnp.concatenate([ref[which, :, columns] for which in range(4)], axis=1)
            if part == 0:
                out_bias_full[...] = joined[slot_count : slot_count + 1]
            for values, out in ((joined, pieces), (ref[mdl_at][:, columns], own_pieces)):
                split = [piece.astype(f32) for piece in split_three(values)]
                out[part] = jnp.concatenate(split + [jnp.zeros_like(values)], axis=0).astype(bf16)

    modulation = total_of(parts, mod_parts, mod_slots)
    mod_out[mdl_at] = jnp.concatenate(
        [add_bias(part, modulation[:, part * local_width : (part + 1) * local_width]) for part in range(2)], axis=1
    )
    mods.start(lambda other: mod_out.at[mdl_at], mod_out)
    token_quad.start(range(2, chunks))
    for chunk in range(2):
        token_quad.hand(chunk)
    head_line.forward(2)
    late_shares.start(lambda other: late_parts.at[other], late_slots)
    mods.wait_recv(lambda other: mod_out.at[mdl_at], mod_out)
    cot_quad.start(range(chunks))
    place_pieces(0, mod_out)
    for chunk in range(2, chunks):
        token_quad.hand(chunk)
    head_line.forward(3)
    for line in unit_lines:
        line.start()
    modulation = total_of(late_shares, late_parts, late_slots)
    late_out[mdl_at] = jnp.concatenate(
        [add_bias(part + 2, modulation[:, part * local_width : (part + 1) * local_width]) for part in range(4)], axis=1
    )
    late_mods.start(lambda other: late_out.at[mdl_at], late_out)
    for chunk in range(chunks):
        token_quad.arrive_rest(chunk)
    own_copies[0].wait()
    own_copies[2].wait()
    head_line.arrive_across()
    qkv_full[...] = head_full[:, : 3 * local_width]
    out_full[...] = head_full[:, 3 * local_width :]

    def span(chunk):
        return pl.ds(pl.multiple_of(chunk * size, 128), size)

    def project(chunk, carry):
        here = span(chunk)
        joined = jnp.concatenate([token_blocks[at, here, :] for at in range(4)], axis=1)
        tokens_full[here, :] = joined
        token_rows = joined.astype(f32)
        hot_now = hot[here, :]
        normed, inverse = centre(token_rows)
        stats[here, 0:1] = jnp.mean(token_rows, axis=1, keepdims=True)
        stats[here, 1:2] = inverse
        scale = mm(hot_now, pieces[1], ((1,), (0,)))
        mod_one[here, :] = (normed * (1.0 + scale) + mm(hot_now, pieces[0], ((1,), (0,)))).astype(bf16)
        projected = (mm(mod_one[here, :], qkv_full[...], ((1,), (0,))) + qkv_bias).astype(bf16)
        for head in range(heads):
            for kind, ref in enumerate((q_heads, k_heads, v_heads)):
                start = kind * local_width + head * head_width
                ref[head, here, :] = projected[:, start : start + head_width]
        forward_units(chunk, tuple((part + 1, part) for part in range(unit_pieces)))
        return carry

    lax.fori_loop(0, chunks, project, 0)
    for head in range(heads):
        v_flip[head] = v_heads[head].T

    def attend_step(at, carry):
        chunk = lax.div(at, heads)
        head = lax.rem(at, heads)
        here = span(chunk)
        scores = mm(k_heads[head], q_heads[head, here, :], ((1,), (1,)))
        same = stats[:, 2:3] == seg_row[0:1, here]
        scores = jnp.where(same, scores * score_scale, unseen)
        column_max = jnp.max(scores, axis=0, keepdims=True)
        terms = jnp.exp(scores - column_max)
        total = jnp.sum(terms, axis=0, keepdims=True)
        logsum[pl.ds(head, 1), here] = column_max + jnp.log(total)
        probs = (terms * (1.0 / total)).astype(bf16)
        att_heads[head] = mm(v_flip[head], probs, ((1,), (0,))).T

        @pl.when(head == heads - 1)
        def _():
            joined = jnp.concatenate([att_heads[which] for which in range(heads)], axis=1)
            attended[here, :] = (joined * mm(hot[here, :], head_rows[...], ((1,), (0,)))).astype(bf16)
            branch_part[here, :] = mm(attended[here, :], out_full[...], ((1,), (1,))).astype(bf16)
            branch.first(chunk)
            pl.when(chunk >= 2)(lambda: branch.third(chunk - 2))

        @pl.when((head == 0) & (chunk >= 1))
        def _():
            branch.second(chunk - 1)

        @pl.when(head == 1)
        def _():
            cot_quad.hand(chunk)

        forward_units(at, ((1, 3), (5, 4), (9, 5), (12, 6), (16, 7), (19, 8)))
        return carry

    lax.fori_loop(0, chunks * heads, attend_step, 0)
    branch.second(chunks - 1)
    late_mods.wait_recv(lambda other: late_out.at[mdl_at], late_out)
    place_pieces(2, late_out)
    branch.third(chunks - 2)
    branch.third(chunks - 1)
    for chunk in range(chunks):
        branch.fourth(chunk)
    for chunk in range(chunks):
        cot_quad.arrive_rest(chunk)
    for line in unit_lines:
        line.arrive_across()
    small.wait_send(lambda other: small_own, small_all)
    times.wait_send(lambda other: time_own, time_all)
    conds.wait_send(lambda other: cond_blocks.at[mdl_at], cond_blocks)
    parts.wait_send(lambda other: mod_parts.at[other], mod_slots)
    mods.wait_send(lambda other: mod_out.at[mdl_at], mod_out)
    late_shares.wait_send(lambda other: late_parts.at[other], late_slots)
    late_mods.wait_send(lambda other: late_out.at[mdl_at], late_out)
    head_line.wait_send()
    for line in unit_lines:
        line.wait_send()
    token_quad.wait_send()
    cot_quad.wait_send()
    for chunk in range(chunks):
        branch.wait_send(chunk)
    own_copies[1].wait()
    own_copies[3].wait()


def front(
    feats_own, class_flip, time_weight, ada_parts, ada_bias, qv_bias, bias_table, qkv_parts, out_flip, up_own, down_flip, token_flip,
    cot_flip, lengths, padding, labels, masks, keep_table, heads, tok_count,
):
    slots = feats_own.shape[0]
    freq_rows, local_width = time_weight.shape
    own_rows, units = up_own.shape
    mod_width = ada_parts.shape[0] * local_width
    rows = token_flip.shape[1]
    small_width = -(-(feats_own.shape[1] + local_width + 1) // 128) * 128
    head_width_all, unit_width = 4 * local_width, 2 * units
    head_width = local_width // heads
    chunks = 5
    size = rows // chunks
    whole = own_rows * tok_count
    dma = pltpu.SemaphoreType.DMA
    vmem = pl.BlockSpec(memory_space=pltpu.VMEM)
    anywhere = pl.BlockSpec(memory_space=pl.ANY)
    scalar = pl.BlockSpec(memory_space=pltpu.SMEM)
    early, late = 2 * local_width, mod_width - 2 * local_width
    low = lambda *shape: pltpu.VMEM(shape, bf16)
    shape = jax.ShapeDtypeStruct
    head_shape = shape((heads, rows, head_width), bf16)
    return pl.pallas_call(
        front_kernel,
        out_shape=(
            shape((tok_count, slots, small_width), f32),
            shape((tok_count * slots, local_width), f32),
            shape((tok_count * slots, own_rows), bf16),
            shape((1, whole), f32),
            shape((6, 4 * slots, whole), bf16),
            shape((6, 4 * slots, local_width), bf16),
            shape((rows, 4 * slots), bf16),
            shape((rows, 4 * slots), bf16),
            shape((4 * slots, local_width), bf16),
            shape((4 * slots, units), bf16),
            shape((slots, rows), f32),
            shape((whole, unit_width), bf16),
            shape((4, rows, local_width), bf16),
            shape((rows, whole), bf16),
            shape((whole, 3 * local_width), bf16),
            shape((whole, local_width), bf16),
            shape((rows, whole), bf16),
            shape((rows, 128), f32),
            head_shape,
            head_shape,
            head_shape,
            shape((heads, rows), f32),
            shape((rows, local_width), bf16),
            shape((rows, whole), bf16),
            shape((rows, local_width), bf16),
            shape((rows, local_width), bf16),
            shape((1, local_width), f32),
            shape((1, units), f32),
            shape((1, local_width), f32),
        ),
        in_specs=[vmem] * 13 + [scalar] * 3 + [vmem] * 2,
        out_specs=(vmem,) * 11 + (anywhere,) * 2 + (vmem,) * 16,
        scratch_shapes=[
            pltpu.VMEM((slots, small_width), f32),
            low(own_rows, head_width_all),
            low(own_rows, unit_width),
            low(whole, head_width_all),
            low(4, rows, local_width),
            low(tok_count, freq_rows, local_width),
            low(4, tok_count * slots, local_width),
            pltpu.VMEM((tok_count, slots, early), f32),
            pltpu.VMEM((tok_count, slots, early), f32),
            pltpu.VMEM((4, slots, early), f32),
            pltpu.VMEM((tok_count, slots, late), f32),
            pltpu.VMEM((tok_count, slots, late), f32),
            pltpu.VMEM((4, slots, late), f32),
            pltpu.VMEM((slots, 128), f32),
            low(heads, head_width, rows),
            pltpu.VMEM((heads, size, head_width), f32),
            low(rows, whole),
            low(chunks, size // 2, whole),
            low(chunks, size // 2, whole),
            low(chunks, size // 2, whole),
            dma((tok_count,)),
            dma((tok_count,)),
            dma((tok_count,)),
            dma((tok_count,)),
            dma((4,)),
            dma((4,)),
            dma((tok_count,)),
            dma((tok_count,)),
            dma((4,)),
            dma((4,)),
            dma((tok_count,)),
            dma((tok_count,)),
            dma((4,)),
            dma((4,)),
            dma((4, 3, tok_count)),
            dma((4, tok_count)),
            dma((2, 3, chunks)),
            dma((2, 4, chunks)),
            dma((3, chunks)),
            dma((3, chunks)),
            dma((4,)),
        ],
        compiler_params=pltpu.CompilerParams(collective_id=0, has_side_effects=True, vmem_limit_bytes=63 * 2**20),
    )(
        feats_own, class_flip, time_weight, ada_parts, ada_bias, qv_bias, bias_table, qkv_parts, out_flip, up_own, down_flip, token_flip,
        cot_flip, lengths, padding, labels, masks, keep_table,
    )


def feed_kernel(
    branch_full,
    tokens_full,
    cot_blocks,
    hot,
    hot_keep,
    pieces,
    out_bias,
    unit_full,
    up_bias,
    chan_rows,
    mlp_part,
    two_full,
    unit_grads,
    up_bias_grad,
    mlp_sums,
    token_buf,
    cot_buf,
    mod_rows,
    gup_rows,
    hid_rows,
    gmlp_rows,
    two_part,
    mlp_buf,
    near_in,
    own_sum,
    far_in,
    sends,
    recvs,
    load_sems,
    store_sems,
):
    mdl_at = lax.axis_index("mdl")
    rows, width = two_full.shape
    chunks = near_in.shape[0]
    size = rows // chunks
    units = up_bias.shape[1]
    local_width = cot_blocks.shape[2]
    greet_quad(mdl_at)
    twos = RowReduce(mdl_at, two_part, near_in, own_sum, far_in, two_full, sends, recvs)

    def span(chunk):
        return pl.ds(pl.multiple_of(chunk * size, 128), size)

    def loads(chunk, slot):
        return (
            pltpu.make_async_copy(tokens_full.at[span(chunk), :], token_buf.at[slot], load_sems.at[0, slot]),
            pltpu.make_async_copy(cot_blocks.at[:, span(chunk), :], cot_buf.at[slot], load_sems.at[1, slot]),
        )

    def store(chunk, slot):
        return pltpu.make_async_copy(mlp_buf.at[slot], mlp_part.at[:, span(chunk), :], store_sems.at[slot])

    for copy in loads(0, 0):
        copy.start()
    up_bias_grad[...] = jnp.zeros_like(up_bias_grad)
    mlp_sums[...] = jnp.zeros_like(mlp_sums)

    def step(chunk, carry):
        slot = lax.rem(chunk, 2)

        @pl.when(chunk + 1 < chunks)
        def _():
            for copy in loads(chunk + 1, 1 - slot):
                copy.start()

        for copy in loads(chunk, slot):
            copy.wait()
        here = span(chunk)
        hot_now = hot[here, :]

        def spread(part):
            return mm(hot_now, pieces[part], ((1,), (0,)))

        token_rows = token_buf[slot].astype(f32)
        middle = token_rows + spread(2) * (branch_full[here, :].astype(f32) + out_bias[...])
        normed, inverse = centre(middle)
        mod_rows[here, :] = (normed * (1.0 + spread(4)) + spread(3)).astype(bf16)
        up_pre = mm(mod_rows[here, :], unit_full[:, :units], ((1,), (0,))) + up_bias[...]
        bend = math.sqrt(2.0 / math.pi)
        square = up_pre * up_pre
        turn = jnp.tanh(bend * up_pre * (1.0 + 0.044715 * square))
        chan = mm(hot_now, chan_rows[...], ((1,), (0,)))
        hid_rows[here, :] = (0.5 * up_pre * (1.0 + turn) * chan).astype(bf16)
        slope = (0.5 * (1.0 + turn) + 0.5 * up_pre * (1.0 - turn * turn) * (bend * (1.0 + 3.0 * 0.044715 * square))) * chan

        @pl.when(chunk >= 2)
        def _():
            store(chunk - 2, slot).wait()

        mlp_rows = mm(hid_rows[here, :], unit_full[:, units:], ((1,), (1,))).astype(bf16)
        for at in range(4):
            mlp_buf[slot, at] = mlp_rows[:, at * local_width : (at + 1) * local_width]
        store(chunk, slot).start()
        cot_rows = jnp.concatenate([cot_buf[slot, at] for at in range(4)], axis=1).astype(f32)
        grad_mlp = (cot_rows * mm(hot_keep[here, :], pieces[5], ((1,), (0,)))).astype(bf16)
        gmlp_rows[here, :] = grad_mlp
        mlp_sums[...] += jnp.sum(grad_mlp.astype(f32), axis=0, keepdims=True)
        grad_up = (mm(gmlp_rows[here, :], unit_full[:, units:], ((1,), (0,))) * slope).astype(bf16)
        gup_rows[here, :] = grad_up
        up_bias_grad[...] += jnp.sum(grad_up.astype(f32), axis=0, keepdims=True)
        two_part[here, :] = mm(gup_rows[here, :], unit_full[:, :units], ((1,), (1,))).astype(bf16)
        twos.first(chunk)
        pl.when(chunk >= 1)(lambda: twos.second(chunk - 1))
        pl.when(chunk >= 2)(lambda: twos.third(chunk - 2))
        return carry

    lax.fori_loop(0, chunks, step, 0)
    twos.second(chunks - 1)
    third = width // 3

    def grads(index, carry):
        at = pl.ds(pl.multiple_of(index * third, 128), third)
        unit_grads[at, :units] = mm(mod_rows[:, at], gup_rows[...], ((0,), (0,))).astype(bf16)
        unit_grads[at, units:] = mm(gmlp_rows[:, at], hid_rows[...], ((0,), (0,))).astype(bf16)
        pl.when(index == 1)(lambda: twos.third(chunks - 2))
        return carry

    lax.fori_loop(0, 3, grads, 0)
    twos.third(chunks - 1)
    for chunk in range(chunks):
        twos.fourth(chunk)
        twos.wait_send(chunk)
    store(chunks - 2, (chunks - 2) % 2).wait()
    store(chunks - 1, (chunks - 1) % 2).wait()


def feed(branch_full, tokens_full, cot_blocks, hot, hot_keep, pieces, out_bias, unit_full, up_bias, chan_rows):
    rows, width = branch_full.shape
    units = up_bias.shape[1]
    local_width = cot_blocks.shape[2]
    chunks = 5
    size = rows // chunks
    dma = pltpu.SemaphoreType.DMA
    vmem = pl.BlockSpec(memory_space=pltpu.VMEM)
    anywhere = pl.BlockSpec(memory_space=pl.ANY)
    low = lambda *shape: pltpu.VMEM(shape, bf16)
    return pl.pallas_call(
        feed_kernel,
        out_shape=(
            jax.ShapeDtypeStruct((4, rows, local_width), bf16),
            jax.ShapeDtypeStruct((rows, width), bf16),
            jax.ShapeDtypeStruct((width, 2 * units), bf16),
            jax.ShapeDtypeStruct((1, units), f32),
            jax.ShapeDtypeStruct((1, width), f32),
        ),
        in_specs=[vmem, anywhere, anywhere] + [vmem] * 7,
        out_specs=(anywhere, vmem, vmem, vmem, vmem),
        scratch_shapes=[
            low(2, size, width),
            low(2, 4, size, local_width),
            low(rows, width),
            low(rows, units),
            low(rows, units),
            low(rows, width),
            low(rows, width),
            low(2, 4, size, local_width),
            low(chunks, size // 2, width),
            low(chunks, size // 2, width),
            low(chunks, size // 2, width),
            dma((3, chunks)),
            dma((3, chunks)),
            dma((2, 2)),
            dma((2,)),
        ],
        compiler_params=pltpu.CompilerParams(collective_id=2, has_side_effects=True, vmem_limit_bytes=63 * 2**20),
    )(branch_full, tokens_full, cot_blocks, hot, hot_keep, pieces, out_bias, unit_full, up_bias, chan_rows)


class ColumnReduce:
    def __init__(self, mdl_at, source, own_part, far_part, near_in, far_out, far_in, sends, recvs, size):
        self.source, self.own_part, self.far_part = source, own_part, far_part
        self.near_in, self.far_out, self.far_in = near_in, far_out, far_in
        self.sends, self.recvs, self.size = sends, recvs, size
        self.near_at = mdl_at + 1 - 2 * lax.rem(mdl_at, 2)
        self.near_far = lax.rem(self.near_at + 2, 4)
        self.near = peer(mdl=self.near_at)
        self.far = peer(mdl=lax.rem(mdl_at + 2, 4))

    def rows(self, chunk):
        return pl.ds(pl.multiple_of(chunk * self.size, 128), self.size)

    def near_copy(self, chunk, which):
        block = self.near_far if which else self.near_at
        return remote(
            self.source.at[block, self.rows(chunk), :],
            self.near_in.at[which, self.rows(chunk), :],
            self.sends.at[which, chunk],
            self.recvs.at[which, chunk],
            self.near,
        )

    def far_copy(self, chunk):
        here = self.rows(chunk)
        return remote(self.far_out.at[here, :], self.far_in.at[here, :], self.sends.at[2, chunk], self.recvs.at[2, chunk], self.far)

    def first(self, chunk):
        self.near_copy(chunk, 1).start()
        self.near_copy(chunk, 0).start()

    def second(self, chunk):
        here = self.rows(chunk)
        self.near_copy(chunk, 1).wait_recv()
        self.far_out[here, :] = (self.far_part[here, :].astype(f32) + self.near_in[1, here, :].astype(f32)).astype(bf16)
        self.far_copy(chunk).start()

    def third(self, chunk):
        here = self.rows(chunk)
        self.near_copy(chunk, 0).wait_recv()
        self.far_copy(chunk).wait_recv()
        return self.own_part[here, :].astype(f32) + self.near_in[0, here, :].astype(f32) + self.far_in[here, :].astype(f32)

    def wait_send(self, chunk):
        self.near_copy(chunk, 1).wait_send()
        self.near_copy(chunk, 0).wait_send()
        self.far_copy(chunk).wait_send()


class LineScatter:
    def __init__(self, tok_at, unit_grads, head_grads, unit_pieces, own_buf, own_sems, cross_in, passed, sends, recvs):
        self.tok_at, self.unit_grads, self.head_grads, self.unit_pieces = tok_at, unit_grads, head_grads, unit_pieces
        self.own_buf, self.own_sems = own_buf, own_sems
        self.cross_in, self.passed = cross_in, passed
        self.sends, self.recvs = sends, recvs
        self.pieces, _, self.rows, self.piece = cross_in.shape
        self.line = lax.div(tok_at, 2)
        self.side = lax.rem(tok_at, 2)
        self.count = 4 * self.pieces
        self.lag = 4

    def at(self, step):
        turn = lax.rem(step, 4)
        return lax.div(step, 4), jnp.where(turn == 0, 0, jnp.where(turn == 1, 3, turn - 1))

    def shard(self, grads, owner, piece):
        columns = pl.ds(pl.multiple_of(piece * self.piece, 128), self.piece)
        return grads.at[pl.ds(pl.multiple_of(owner * self.rows, 16), self.rows), columns]

    def cross_copy(self, grads, piece, part, place):
        return remote(
            self.shard(grads, 2 * place + 1 - self.side, piece),
            self.cross_in.at[part, place],
            self.sends.at[part, 0, place],
            self.recvs.at[part, 0, place],
            peer(tok=self.tok_at + 1 - 2 * self.side),
        )

    def down_copy(self, part, place):
        return remote(
            self.cross_in.at[part, place],
            self.passed.at[part, place],
            self.sends.at[part, 1, place],
            self.recvs.at[part, 1, place],
            peer(tok=self.tok_at - 2),
        )

    def up_copy(self, part, place, line):
        slot = jnp.where(line == place, 4, place)
        return remote(
            self.cross_in.at[part, place],
            self.passed.at[part, slot],
            self.sends.at[part, 1, place],
            self.recvs.at[part, 2, place],
            peer(tok=self.tok_at + 2),
        )

    def each_cross(self, first, last, act):
        def step(index, carry):
            part, place = self.at(index)
            if last <= 4 * self.unit_pieces:
                act(self.cross_copy(self.unit_grads, part, part, place))
            else:
                act(self.cross_copy(self.head_grads, part - self.unit_pieces, part, place))
            return carry

        lax.fori_loop(first, last, step, 0)

    def start(self, first, last):
        self.each_cross(first, last, lambda copy: copy.start())

    def own_copy(self, grads, piece, step, place):
        slot = lax.rem(step, 2)
        return pltpu.make_async_copy(self.shard(grads, 2 * place + self.side, piece), self.own_buf.at[slot], self.own_sems.at[slot])

    def load(self, step):
        part, place = self.at(step)
        pl.when(part < self.unit_pieces)(lambda: self.own_copy(self.unit_grads, part, step, place).start())
        pl.when(part >= self.unit_pieces)(
            lambda: self.own_copy(self.head_grads, part - self.unit_pieces, step, place).start()
        )

    def add(self, part, place, values):
        self.cross_in[part, place] = (values.astype(f32) + self.cross_in[part, place].astype(f32)).astype(bf16)

    def serve(self, step):
        @pl.when(step < self.count)
        def _():
            part, place = self.at(step)
            self.own_copy(self.unit_grads, 0, step, 0).wait()
            pl.when(step + 1 < self.count)(lambda: self.load(step + 1))
            self.cross_copy(self.unit_grads, 0, part, place).wait_recv()
            self.add(part, place, self.own_buf[lax.rem(step, 2)])

        for hop in range(3):
            before = step - hop * self.lag
            part, place = self.at(jnp.maximum(before, 0))
            real = (before >= 0) & (before < self.count)
            down = real & (self.line > place) & (self.line == 3 - hop)
            up = real & (self.line < place) & (self.line == hop)
            if hop:
                pl.when(down)(lambda part=part, place=place: self.down_copy(part, place).wait_recv())
                pl.when(up)(lambda part=part, place=place: self.up_copy(part, place, self.line).wait_recv())
                pl.when(down | up)(lambda part=part, place=place: self.add(part, place, self.passed[part, place]))
            pl.when(down)(lambda part=part, place=place: self.down_copy(part, place).start())
            pl.when(up)(lambda part=part, place=place: self.up_copy(part, place, self.line + 1).start())

    def serve_range(self, first, last):
        def step(index, carry):
            self.serve(index)
            return carry

        lax.fori_loop(first, last, step, 0)

    def finish(self, part, out, piece):
        own = self.line
        columns = pl.ds(pl.multiple_of(piece * self.piece, 128), self.piece)
        out[:, columns] = self.cross_in[part, own].astype(f32)

        @pl.when(self.line < 3)
        def _():
            self.down_copy(part, own).wait_recv()
            out[:, columns] += self.passed[part, own].astype(f32)

        @pl.when(self.line > 0)
        def _():
            self.up_copy(part, own, self.line).wait_recv()
            out[:, columns] += self.passed[part, 4].astype(f32)

    def wait_send(self):
        self.each_cross(0, 4 * self.unit_pieces, lambda copy: copy.wait_send())
        self.each_cross(4 * self.unit_pieces, self.count, lambda copy: copy.wait_send())

        def step(index, carry):
            part, place = self.at(index)
            pl.when(self.line > place)(lambda: self.down_copy(part, place).wait_send())
            pl.when(self.line < place)(lambda: self.up_copy(part, place, self.line + 1).wait_send())
            return carry

        lax.fori_loop(0, self.count, step, 0)


def own_block(mdl_at, values, width, act):
    for at in range(4):
        pl.when(mdl_at == at)(lambda at=at: act(values[:, at * width : (at + 1) * width]))


def rear_kernel(
    two_full,
    branch_full,
    tokens_full,
    cot_blocks,
    mlp_blocks,
    unit_grads,
    q_any,
    k_any,
    v_any,
    mod_any,
    qkv_any,
    out_any,
    att_any,
    hot,
    hot_keep,
    pieces,
    own_pieces,
    out_bias_full,
    out_bias,
    down_bias,
    head_rows,
    logsum,
    seg_row,
    tokens,
    cotangent,
    stats_one,
    up_bias_sum,
    mlp_sum,
    ada_parts,
    cond_own,
    embedding,
    output,
    grad_flip,
    up_out,
    down_out,
    qkv_grads,
    out_grads,
    gmod_sum,
    grad_ada,
    ada_bias_grad,
    grad_embed,
    head_grads,
    gmod_all,
    token_buf,
    cot_buf,
    two_buf,
    branch_buf,
    q_heads,
    k_heads,
    v_heads,
    mod_buf,
    qkv_full,
    out_full,
    attended,
    g_heads,
    key_flip,
    dk_sum,
    dv_sum,
    out_sum,
    attn_sums,
    branch_own,
    two_own,
    mlp_own,
    stats_two,
    cross_in,
    passed,
    own_buf,
    qkv_rows,
    full_grads,
    col_blocks,
    col_near,
    col_out,
    col_far,
    gmod_own,
    gmod_low,
    row_sums,
    part_own,
    part_slots,
    cond_slots,
    load_sems,
    fetch_sems,
    mod_sems,
    part_sems,
    own_sems,
    line_sends,
    line_recvs,
    mlp_sends,
    mlp_recvs,
    one_sends,
    one_recvs,
    row_send,
    row_recv,
    gmod_send,
    gmod_recv,
    part_send,
    part_recv,
    cond_send,
    cond_recv,
    free_sem,
):
    tok_at = lax.axis_index("tok")
    mdl_at = lax.axis_index("mdl")
    far_at = lax.rem(mdl_at + 2, 4)
    near_at = mdl_at + 1 - 2 * lax.rem(mdl_at, 2)
    tok_count, slots = gmod_all.shape[0], gmod_all.shape[1]
    rows, local_width = tokens.shape
    width = qkv_full.shape[0]
    units = up_out.shape[1]
    own_rows = head_grads.shape[0]
    heads, _, head_width = q_heads.shape
    chunks = mlp_sends.shape[1]
    size = rows // chunks
    score_scale = 1.0 / math.sqrt(head_width)
    third = width // 3
    piece = cross_in.shape[3]
    unit_pieces = 2 * units // piece

    def span(chunk):
        return pl.ds(pl.multiple_of(chunk * size, 128), size)

    def loads(chunk, slot):
        return (
            pltpu.make_async_copy(tokens_full.at[span(chunk), :], token_buf.at[slot], load_sems.at[0, slot]),
            pltpu.make_async_copy(cot_blocks.at[:, span(chunk), :], cot_buf.at[slot], load_sems.at[1, slot]),
            pltpu.make_async_copy(two_full.at[span(chunk), :], two_buf.at[slot], load_sems.at[2, slot]),
            pltpu.make_async_copy(branch_full.at[span(chunk), :], branch_buf.at[slot], load_sems.at[3, slot]),
        )

    def mod_load(index):
        at = pl.ds(pl.multiple_of(index * third, 128), third)
        slot = lax.rem(index, 2)
        return pltpu.make_async_copy(mod_any.at[:, at], mod_buf.at[slot], mod_sems.at[slot])

    fetches = [
        pltpu.make_async_copy(source, target, fetch_sems.at[index])
        for index, (source, target) in enumerate(
            (
                (out_any, out_full),
                (att_any, attended),
                (k_any, k_heads),
                (q_any, q_heads),
                (v_any, v_heads),
                (qkv_any, qkv_full),
            )
        )
    ]
    for copy in loads(0, 0):
        copy.start()
    for copy in fetches[:3]:
        copy.start()
    greet(tok_at, mdl_at, tok_count, 4)
    line = LineScatter(
        tok_at, unit_grads, full_grads, unit_pieces, own_buf, own_sems, cross_in, passed, line_sends, line_recvs
    )

    mlps = ColumnReduce(
        mdl_at, mlp_blocks, col_blocks.at[mdl_at], col_blocks.at[far_at], col_near, col_out, col_far, mlp_sends, mlp_recvs, size
    )
    ones = ColumnReduce(
        mdl_at, col_blocks, col_blocks.at[mdl_at], col_blocks.at[far_at], col_near, col_out, col_far, one_sends, one_recvs, size
    )
    line.start(0, 4 * unit_pieces)
    for chunk in range(chunks):
        mlps.first(chunk)
    part_loads = [
        pltpu.make_async_copy(mlp_blocks.at[mdl_at], col_blocks.at[mdl_at], part_sems.at[0]),
        pltpu.make_async_copy(mlp_blocks.at[far_at], col_blocks.at[far_at], part_sems.at[1]),
    ]
    for copy in part_loads:
        copy.start()
    line.load(0)
    for copy in fetches[3:]:
        copy.start()
    mod_load(0).start()
    mod_load(1).start()
    attn_sums[...] = jnp.zeros_like(attn_sums)
    out_sum[...] = jnp.zeros_like(out_sum)
    for copy in fetches[:3]:
        copy.wait()
    for head in range(heads):
        key_flip[head] = k_heads[head].T
    for copy in part_loads:
        copy.wait()

    def back_step(chunk, carry):
        slot = lax.rem(chunk, 2)

        @pl.when(chunk + 1 < chunks)
        def _():
            for copy in loads(chunk + 1, 1 - slot):
                copy.start()

        for copy in loads(chunk, slot):
            copy.wait()
        mlps.second(chunk)
        here = span(chunk)
        hot_now = hot[here, :]

        def spread(part):
            return mm(hot_now, pieces[part], ((1,), (0,)))

        gate_one = spread(2)
        middle = token_buf[slot].astype(f32) + gate_one * (branch_buf[slot].astype(f32) + out_bias_full[...])
        row_mean = jnp.mean(middle, axis=1, keepdims=True)
        normed, inverse = centre(middle)
        grad_norm = two_buf[slot].astype(f32) * (1.0 + spread(4))
        mean_one = jnp.mean(grad_norm, axis=1, keepdims=True)
        mean_two = jnp.mean(grad_norm * normed, axis=1, keepdims=True)
        cot_rows = jnp.concatenate([cot_buf[slot, at] for at in range(4)], axis=1).astype(f32)
        grad_middle = cot_rows + inverse * (grad_norm - mean_one - normed * mean_two)
        grad_attn = (grad_middle * gate_one).astype(bf16)
        attn_sums[...] += jnp.sum(grad_attn.astype(f32), axis=0, keepdims=True)
        grad_att = mm(grad_attn, out_full[...], ((1,), (0,))).astype(bf16).astype(f32)
        grad_att = (grad_att * mm(hot_now, head_rows[...], ((1,), (0,)))).astype(bf16)
        for head in range(heads):
            g_heads[head, here, :] = grad_att[:, head * head_width : (head + 1) * head_width]
        out_sum[...] += mm(grad_attn, attended[here, :], ((0,), (0,)))
        for column, value in enumerate((row_mean, inverse, mean_one, mean_two)):
            stats_two[here, column : column + 1] = value

        def keep(ref):
            def act(part):
                ref[here, :] = part

            return act

        own_block(mdl_at, branch_buf[slot], local_width, keep(branch_own))
        own_block(mdl_at, two_buf[slot], local_width, keep(two_own))
        pl.when(chunk >= 1)(lambda: line.serve(chunk - 1))
        return carry

    lax.fori_loop(0, chunks, back_step, 0)
    served = chunks - 1
    for copy in fetches[3:]:
        copy.wait()

    def attend_step(at, carry):
        head = lax.div(at, chunks)
        chunk = lax.rem(at, chunks)
        here = span(chunk)

        @pl.when(chunk == 0)
        def _():
            dk_sum[...] = jnp.zeros_like(dk_sum)
            dv_sum[...] = jnp.zeros_like(dv_sum)

        query = q_heads[head, here, :]
        grad = g_heads[head, here, :]
        scores = mm(k_heads[head], query, ((1,), (1,)))
        same = stats_one[:, 2:3] == seg_row[0:1, here]
        probs = jnp.exp(jnp.where(same, scores * score_scale - logsum[pl.ds(head, 1), here], unseen))
        grad_prob = mm(v_heads[head], grad, ((1,), (1,)))
        dv_sum[...] += mm(probs.astype(bf16), grad, ((1,), (0,)))
        product = probs * grad_prob
        grad_scores = (product - probs * jnp.sum(product, axis=0, keepdims=True)).astype(bf16)
        dk_sum[...] += mm(grad_scores, query, ((1,), (0,)))
        flipped = mm(key_flip[head], grad_scores, ((1,), (0,)))
        q_heads[head, here, :] = (flipped.T * score_scale).astype(bf16)

        @pl.when(chunk == chunks - 1)
        def _():
            k_heads[head] = (dk_sum[...] * score_scale).astype(bf16)
            v_heads[head] = dv_sum[...].astype(bf16)

        @pl.when(at < chunks)
        def _():
            mlp_own[span(at), :] = mlps.third(at).astype(bf16)

        pl.when(lax.rem(at, 2) == 1)(lambda: line.serve(served + lax.div(at, 2)))
        return carry

    lax.fori_loop(0, chunks * heads, attend_step, 0)
    served += heads * chunks // 2
    for chunk in range(chunks):
        mlps.wait_send(chunk)
    for other in (near_at, far_at):
        pl.semaphore_signal(free_sem, inc=1, device_id=peer(mdl=other), device_id_type=pl.DeviceIdType.MESH)

    gmod_own[...] = jnp.zeros_like(gmod_own)
    up_sum = up_bias_sum[...]
    split = 6 * local_width - 3 * local_width
    gmod_own[slots - 2 : slots - 1, 3 * local_width :] = up_sum[:, :split]
    gmod_own[slots - 1 : slots, : units - split] = up_sum[:, split:]

    def keep_sum(row, start):
        def act(part):
            gmod_own[row : row + 1, start : start + local_width] = part

        return act

    own_block(mdl_at, attn_sums[...], local_width, keep_sum(slots - 2, 2 * local_width))
    own_block(mdl_at, mlp_sum[...], local_width, keep_sum(slots - 1, units - split))

    def gather_rows(chunk, carry):
        here = span(chunk)
        joined = jnp.concatenate(
            [part[head, here, :] for part in (q_heads, k_heads, v_heads) for head in range(heads)], axis=1
        )
        qkv_rows[here, :] = joined
        total = jnp.sum(joined.astype(f32), axis=0, keepdims=True)
        gmod_own[slots - 2 : slots - 1, :local_width] += total[:, :local_width]
        gmod_own[slots - 2 : slots - 1, local_width : 2 * local_width] += total[:, 2 * local_width :]
        return carry

    lax.fori_loop(0, chunks, gather_rows, 0)
    line.serve_range(served, served + 2)
    served += 2
    pl.semaphore_wait(free_sem, 2)

    def ones_step(chunk, carry):
        here = span(chunk)
        part = mm(qkv_rows[here, :], qkv_full[...], ((1,), (1,))).astype(bf16)
        for at in range(4):
            col_blocks[at, here, :] = part[:, at * local_width : (at + 1) * local_width]
        ones.first(chunk)
        pl.when(chunk >= 1)(lambda: ones.second(chunk - 1))
        pl.when(lax.rem(chunk, 2) == 1)(lambda: line.serve(served + lax.div(chunk, 2)))
        return carry

    lax.fori_loop(0, chunks, ones_step, 0)
    ones.second(chunks - 1)
    served += 2

    def grads(index, carry):
        at = pl.ds(pl.multiple_of(index * third, 128), third)
        mod_load(index).wait()
        weight = mm(mod_buf[lax.rem(index, 2)], qkv_rows[...], ((0,), (0,))).astype(bf16)
        full_grads[at, :] = jnp.concatenate([weight, out_sum[at, :].astype(bf16)], axis=1)
        pl.when(index == 0)(lambda: mod_load(2).start())
        line.serve(served + index)
        return carry

    lax.fori_loop(0, 3, grads, 0)
    line.start(4 * unit_pieces, line.count - 4)
    served += 3
    pick = lax.broadcasted_iota(jnp.int32, (8, local_width), 0)
    first_row = jnp.where(pick == 0, 1.0, 0.0).astype(bf16)
    second_row = jnp.where(pick == 1, 1.0, 0.0).astype(bf16)

    def final_step(chunk, carry):
        here = span(chunk)
        hot_now = hot[here, :]
        crop_now = hot_now[:, :slots]
        keep_now = hot_keep[here, :]

        def spread(part):
            return mm(hot_now, own_pieces[part], ((1,), (0,)))

        token_rows = tokens[here, :].astype(f32)
        branch = branch_own[here, :].astype(f32) + out_bias[...]
        mlp = mlp_own[here, :].astype(f32) + down_bias[...]
        cot_rows = cotangent[here, :].astype(f32)
        grad_two = two_own[here, :].astype(f32)
        middle = token_rows + spread(2) * branch
        output[:, here] = (middle + mm(keep_now, own_pieces[5], ((1,), (0,))) * mlp).T.astype(bf16)
        inverse_two = stats_two[here, 1:2]
        normed_two = (middle - stats_two[here, 0:1]) * inverse_two
        grad_middle = cot_rows + inverse_two * (
            grad_two * (1.0 + spread(4)) - stats_two[here, 2:3] - normed_two * stats_two[here, 3:4]
        )
        grad_flip[:, here] = grad_middle.T
        grad_one = ones.third(chunk)
        normed_one = (token_rows - stats_one[here, 0:1]) * stats_one[here, 1:2]
        grad_norm = grad_one * (1.0 + spread(1))
        total = jnp.zeros((8, size), f32)
        for row, values in ((first_row, grad_norm), (second_row, grad_norm * normed_one)):
            for split in split_two(values):
                total = total + mm(row, split, ((1,), (1,)))
        row_sums[mdl_at, :, here] = total
        terms = (
            (0, crop_now, grad_one),
            (1, crop_now, grad_one * normed_one),
            (2, crop_now, grad_middle * branch),
            (3, crop_now, grad_two),
            (4, crop_now, grad_two * normed_two),
            (5, keep_now[:, :slots], cot_rows * mlp),
        )
        for part, chosen, values in terms:
            high, rest = split_two(values)
            gmod_own[:, part * local_width : (part + 1) * local_width] += mm(chosen, high, ((0,), (0,))) + mm(
                chosen, rest, ((0,), (0,))
            )
        line.serve(served + chunk)
        return carry

    lax.fori_loop(0, chunks, final_step, 0)
    served += chunks
    row_peers = AllToPeers("mdl", mdl_at, 4, row_send, row_recv)
    gmods = AllToPeers("tok", tok_at, tok_count, gmod_send, gmod_recv)
    row_peers.start(lambda other: row_sums.at[mdl_at], row_sums)
    turn = gmod_low.shape[2]
    gmod_low[tok_at] = jnp.zeros_like(gmod_low[tok_at])
    gmod_low[tok_at, :slots, :] = gmod_own[:, :turn].astype(bf16)
    gmod_low[tok_at, slots:, : 6 * local_width - turn] = gmod_own[:, turn:].astype(bf16)
    gmods.start(lambda other: gmod_low.at[tok_at], gmod_low)
    line.start(line.count - 4, line.count)
    line.serve_range(served, served + 3)
    served += 3
    row_peers.wait_recv(lambda other: row_sums.at[mdl_at], row_sums)
    totals = ((row_sums[0] + row_sums[1] + row_sums[2] + row_sums[3]) * (1.0 / width)).T
    for chunk in range(chunks):
        here = pl.ds(chunk * size, size)
        flip = totals[chunk * size : (chunk + 1) * size]
        inverse_one = stats_one[here, 1:2]
        normed_one = (tokens[here, :].astype(f32) - stats_one[here, 0:1]) * inverse_one
        grad_one = col_blocks[mdl_at, here, :].astype(f32) + col_near[0, here, :].astype(f32) + col_far[here, :].astype(f32)
        grad_norm = grad_one * (1.0 + mm(hot[here, :], own_pieces[1], ((1,), (0,))))
        grad_flip[:, here] += (inverse_one * (grad_norm - flip[:, 0:1] - normed_one * flip[:, 1:2])).T
    line.serve_range(served, served + 2)
    served += 2
    gmods.wait_recv(lambda other: gmod_low.at[tok_at], gmod_low)
    for at in range(tok_count):
        gmod_all[at] = jnp.concatenate(
            [gmod_low[at, :slots, :].astype(f32), gmod_low[at, slots:, : 6 * local_width - turn].astype(f32)], axis=1
        )
    gathered = gmod_all[...].reshape(tok_count * slots, gmod_all.shape[2]).astype(bf16)
    columns = [slice(part * local_width, (part + 1) * local_width) for part in range(6)]
    total = mm(gathered[:, columns[0]], ada_parts[0], ((1,), (1,)))
    for part in range(1, 6):
        total = total + mm(gathered[:, columns[part]], ada_parts[part], ((1,), (1,)))
    part_own[...] = total
    owner = lax.div(tok_at, 2)
    half = lax.rem(tok_at, 2)

    def part_copy(source):
        return remote(part_own, part_slots.at[source], part_send.at[0], part_recv.at[source], peer(mdl=owner))

    pl.when(mdl_at != owner)(lambda: part_copy(mdl_at).start())
    cond = cond_own[...]
    crop_total = gmod_all[0]
    for at in range(1, tok_count):
        crop_total = crop_total + gmod_all[at]
    gmod_sum[...] = crop_total
    for part in range(6):
        grad_ada[part] = mm(cond, gathered[:, columns[part]], ((0,), (0,)))
        ada_bias_grad[part : part + 1, :] = jnp.sum(crop_total[: slots - 2, columns[part]], axis=0, keepdims=True)

    def cond_copy(step):
        other = lax.rem(tok_at + step, tok_count)
        return remote(cond_slots.at[half], cond_slots.at[half], cond_send.at[step], cond_recv.at[half], peer(tok=other))

    @pl.when(mdl_at == owner)
    def _():
        total = part_own[...]
        for step in range(1, 4):
            source = lax.rem(mdl_at + step, 4)
            part_copy(source).wait_recv()
            total = total + part_slots[source]
        cond_slots[half] = total
        for step in range(1, tok_count):
            cond_copy(step).start()

    line.serve_range(served, line.count + 2 * line.lag)
    for first, out in ((0, up_out), (unit_pieces // 2, down_out), (unit_pieces, head_grads)):

        def close(index, carry):
            line.finish(first + index, out, index)
            return carry

        lax.fori_loop(0, out.shape[1] // piece, close, 0)

    for part in range(3):
        qkv_grads[part] = head_grads[:, part * local_width : (part + 1) * local_width]
    out_grads[...] = head_grads[:, 3 * local_width :]
    for side in range(2):
        giver = 2 * mdl_at + side

        @pl.when(tok_at != giver)
        def _():
            remote(cond_slots.at[side], cond_slots.at[side], cond_send.at[0], cond_recv.at[side], peer(tok=giver)).wait_recv()

    grad_cond = jnp.concatenate([cond_slots[0], cond_slots[1]], axis=1)
    embed = embedding[...]
    gate = 1.0 / (1.0 + jnp.exp(-embed))
    grad_embed[...] = grad_cond * gate * (1.0 + embed * (1.0 - gate))
    gmods.wait_send(lambda other: gmod_low.at[tok_at], gmod_low)
    row_peers.wait_send(lambda other: row_sums.at[mdl_at], row_sums)
    pl.when(mdl_at != owner)(lambda: part_copy(mdl_at).wait_send())

    @pl.when(mdl_at == owner)
    def _():
        for step in range(1, tok_count):
            cond_copy(step).wait_send()

    line.wait_send()
    for chunk in range(chunks):
        ones.wait_send(chunk)


def rear(
    two_full, branch_full, tokens_full, cot_blocks, mlp_blocks, unit_grads, q_heads, k_heads, v_heads, mod_one, qkv_full, out_full, attended,
    hot, hot_keep, pieces, own_pieces, out_bias_full, out_bias, down_bias, head_rows, logsum, seg_row, tokens, cotangent, stats_one,
    up_bias_sum, mlp_sum, ada_parts, cond_own, embedding, tok_count,
):
    rows, local_width = tokens.shape
    width, three = qkv_full.shape
    units = unit_grads.shape[1] // 2
    own_rows = width // tok_count
    slots = 8
    mod_width = 6 * local_width
    crops = cond_own.shape[0]
    heads, _, head_width = q_heads.shape
    chunks, pieces_count = 5, 9
    size = rows // chunks
    total = three + local_width
    dma = pltpu.SemaphoreType.DMA
    vmem = pl.BlockSpec(memory_space=pltpu.VMEM)
    anywhere = pl.BlockSpec(memory_space=pl.ANY)
    low = lambda *shape: pltpu.VMEM(shape, bf16)
    wide = lambda *shape: pltpu.VMEM(shape, f32)
    shape = jax.ShapeDtypeStruct
    piece = (2 * units + total) // pieces_count
    return pl.pallas_call(
        rear_kernel,
        out_shape=(
            shape((local_width, rows), bf16),
            shape((local_width, rows), f32),
            shape((own_rows, units), f32),
            shape((own_rows, units), f32),
            shape((3, own_rows, local_width), f32),
            shape((own_rows, local_width), f32),
            shape((slots, mod_width), f32),
            shape((6, own_rows, local_width), f32),
            shape((6, local_width), f32),
            shape(embedding.shape, f32),
        ),
        in_specs=[anywhere] * 13 + [vmem] * 18,
        out_specs=(vmem,) * 10,
        scratch_shapes=[
            wide(own_rows, total),
            wide(tok_count, slots, mod_width),
            low(2, size, width),
            low(2, 4, size, local_width),
            low(2, size, width),
            low(2, size, width),
            low(heads, rows, head_width),
            low(heads, rows, head_width),
            low(heads, rows, head_width),
            low(2, rows, width // 3),
            low(width, three),
            low(width, local_width),
            low(rows, local_width),
            low(heads, rows, head_width),
            low(heads, head_width, rows),
            wide(rows, head_width),
            wide(rows, head_width),
            wide(width, local_width),
            wide(1, width),
            low(rows, local_width),
            low(rows, local_width),
            low(rows, local_width),
            wide(rows, 128),
            low(pieces_count, 4, own_rows, piece),
            low(pieces_count, 5, own_rows, piece),
            low(2, own_rows, piece),
            low(rows, three),
            low(width, total),
            low(4, rows, local_width),
            low(2, rows, local_width),
            low(rows, local_width),
            low(rows, local_width),
            wide(slots, mod_width),
            low(tok_count, 2 * slots, -(-mod_width // 256) * 128),
            wide(4, 8, rows),
            wide(crops, own_rows),
            wide(4, crops, own_rows),
            wide(2, crops, own_rows),
            dma((4, 2)),
            dma((6,)),
            dma((2,)),
            dma((2,)),
            dma((2,)),
            dma((pieces_count, 2, 4)),
            dma((pieces_count, 3, 4)),
            dma((3, chunks)),
            dma((3, chunks)),
            dma((3, chunks)),
            dma((3, chunks)),
            dma((4,)),
            dma((4,)),
            dma((tok_count,)),
            dma((tok_count,)),
            dma((1,)),
            dma((4,)),
            dma((tok_count,)),
            dma((2,)),
            pltpu.SemaphoreType.REGULAR,
        ],
        compiler_params=pltpu.CompilerParams(collective_id=1, has_side_effects=True, vmem_limit_bytes=67043328),
    )(
        two_full, branch_full, tokens_full, cot_blocks, mlp_blocks, unit_grads, q_heads, k_heads, v_heads, mod_one, qkv_full, out_full, attended,
        hot, hot_keep, pieces, own_pieces, out_bias_full, out_bias, down_bias, head_rows, logsum, seg_row, tokens, cotangent, stats_one,
        up_bias_sum, mlp_sum, ada_parts, cond_own, embedding,
    )


def on_device(
    tokens,
    cotangent,
    lengths,
    padding,
    timesteps,
    labels,
    head_mask,
    chan_mask,
    keep_mask,
    qkv_weight,
    qv_bias,
    out_weight,
    out_bias,
    up_weight,
    up_bias,
    down_weight,
    down_bias,
    ada_weight,
    ada_bias,
    time_weight,
    class_table,
):
    row_count, slot_count = lengths.shape
    token_count, local_width = tokens.shape
    row_len = token_count // row_count
    heads_here = head_mask.shape[2]
    head_width = local_width // heads_here
    units_here = up_bias.shape[0]
    groups_here = chan_mask.shape[2]
    own_rows = qkv_weight.shape[0]
    full_width = local_width * lax.axis_size("mdl")
    score_scale = 1.0 / math.sqrt(head_width)
    tok_at = lax.axis_index("tok")
    mdl_at = lax.axis_index("mdl")

    def own_cols(full_rows):
        return lax.dynamic_slice_in_dim(full_rows, mdl_at * local_width, local_width, axis=1)

    slots = 8
    tok_count = lax.axis_size("tok")
    freq_rows = time_weight.shape[0]
    freq_count = freq_rows * tok_count
    ada_parts = jnp.transpose(ada_weight, (1, 0, 2))
    feats_own = jnp.pad(timestep_features(timesteps[0], freq_count), ((0, slots - slot_count), (0, 0)))
    lanes = 128
    bias_parts = [
        jnp.pad(out_bias, (0, -local_width % lanes)), jnp.pad(down_bias, (0, -local_width % lanes)), up_bias
    ]
    bias_table = jnp.concatenate(bias_parts).astype(f32)
    bias_table = jnp.pad(bias_table, (0, -bias_table.shape[0] % (8 * lanes))).reshape(-1, lanes)
    masks = jnp.concatenate([head_mask, chan_mask], axis=2)
    (
        small_all,
        embedding,
        cond_own,
        out_bias_full,
        pieces,
        own_pieces,
        hot,
        hot_keep,
        head_rows,
        chan_rows,
        seg_row,
        unit_full,
        cot_blocks,
        tokens_full,
        qkv_full,
        out_full,
        modulated_one,
        stats_one,
        q_heads,
        k_heads,
        v_heads,
        logsum_rows,
        attended,
        branch_low,
        tokens_own,
        cot_own,
        out_row,
        up_row,
        down_row,
    ) = front(
        feats_own, class_table.T, time_weight, ada_parts, ada_bias, qv_bias, bias_table, jnp.transpose(qkv_weight, (1, 0, 2)),
        out_weight.T, up_weight, down_weight.T, tokens.T, cotangent.T, lengths, padding, labels, masks,
        keep_mask.reshape(-1, lanes), heads_here, tok_count,
    )
    all_crops = tok_count * slots
    real_crop = (jnp.arange(all_crops, dtype=jnp.int32) % slots < slot_count)[:, None]
    step_feats = small_all[:, :, :freq_count].reshape(all_crops, freq_count)
    label_all = small_all[:, :, freq_count + local_width].reshape(all_crops).astype(jnp.int32)
    label_hot = ((label_all[:, None] == jnp.arange(class_table.shape[0], dtype=jnp.int32)[None, :]) & real_crop).astype(f32)
    mlp_blocks, two_low, unit_grads, grad_up_bias, mlp_sums = feed(
        branch_low, tokens_full, cot_blocks, hot, hot_keep, pieces, out_bias_full, unit_full, up_row, chan_rows
    )
    output, grad_tokens, grad_up, grad_down, grad_qkv, grad_out, gmod_sum, grad_ada, grad_ada_bias, grad_embed = rear(
        two_low, branch_low, tokens_full, cot_blocks, mlp_blocks, unit_grads, q_heads, k_heads, v_heads, modulated_one, qkv_full, out_full,
        attended, hot, hot_keep, pieces, own_pieces, out_bias_full, out_row, down_row, head_rows,
        logsum_rows, seg_row, tokens_own, cot_own, stats_one, grad_up_bias, mlp_sums, ada_parts, cond_own, embedding, tok_count,
    )
    bias_total = gmod_sum[slot_count:].reshape(-1)
    grad_qv_bias = bias_total[: 2 * local_width].reshape(2, local_width)
    grad_out_bias = bias_total[2 * local_width : 3 * local_width]
    grad_up_bias = bias_total[3 * local_width : 3 * local_width + units_here]
    grad_down_bias = bias_total[3 * local_width + units_here : 4 * local_width + units_here]
    own_feats = lax.dynamic_slice_in_dim(step_feats, tok_at * freq_rows, freq_rows, axis=1)
    grad_time = exact_dot(own_feats.T, grad_embed)
    grad_class = exact_dot(label_hot.T, grad_embed)
    return (
        output.T,
        grad_tokens.T,
        jnp.transpose(grad_qkv, (1, 0, 2)),
        grad_qv_bias,
        grad_out.T,
        grad_out_bias,
        grad_up,
        grad_up_bias,
        grad_down.T,
        grad_down_bias,
        jnp.transpose(grad_ada, (1, 0, 2)),
        grad_ada_bias,
        grad_time,
        grad_class,
    )


def on_device_any(
    tokens,
    cotangent,
    lengths,
    padding,
    timesteps,
    labels,
    head_mask,
    chan_mask,
    keep_mask,
    qkv_weight,
    qv_bias,
    out_weight,
    out_bias,
    up_weight,
    up_bias,
    down_weight,
    down_bias,
    ada_weight,
    ada_bias,
    time_weight,
    class_table,
):
    row_count, slot_count = lengths.shape
    token_count, local_width = tokens.shape
    row_len = token_count // row_count
    heads_here = head_mask.shape[2]
    head_width = local_width // heads_here
    units_here = up_bias.shape[0]
    groups_here = chan_mask.shape[2]
    own_rows = qkv_weight.shape[0]
    full_width = local_width * lax.axis_size("mdl")
    score_scale = 1.0 / math.sqrt(head_width)
    tok_at = lax.axis_index("tok")
    mdl_at = lax.axis_index("mdl")

    def own_cols(full_rows):
        return lax.dynamic_slice_in_dim(full_rows, mdl_at * local_width, local_width, axis=1)

    all_steps = lax.all_gather(jnp.stack([timesteps, labels]), "tok", axis=1, tiled=True)
    time_full = lax.all_gather(time_weight, "tok", axis=0, tiled=True)
    all_crops = all_steps.shape[1] * slot_count
    step_feats = timestep_features(all_steps[0].reshape(all_crops), time_full.shape[0])
    label_hot = (
        all_steps[1].reshape(all_crops)[:, None] == jnp.arange(class_table.shape[0], dtype=jnp.int32)[None, :]
    ).astype(bf16)
    embedding = exact_dot(step_feats, time_full.astype(f32)) + mm(label_hot, class_table, ((1,), (0,)))
    cond_full = gather_cols(jax.nn.silu(embedding).astype(bf16))
    cond_own = lax.dynamic_slice_in_dim(cond_full, tok_at * own_rows, own_rows, axis=1)
    ada_own = ada_weight.reshape(own_rows, 6 * local_width)
    modulation = lax.psum_scatter(
        mm(cond_own, ada_own, ((1,), (0,))), "tok", scatter_dimension=0, tiled=True
    ).reshape(slot_count, 6, local_width) + ada_bias.astype(f32)[None]
    mod_full = lax.all_gather(modulation, "mdl", axis=2, tiled=True)

    head_shard = jnp.concatenate([qkv_weight.reshape(own_rows, 3 * local_width), out_weight.T], axis=1)
    unit_shard = jnp.concatenate([up_weight, down_weight.T], axis=1)
    head_full = lax.all_gather(head_shard, "tok", axis=0, tiled=True)
    unit_full = lax.all_gather(unit_shard, "tok", axis=0, tiled=True)
    qkv_full, out_full = head_full[:, : 3 * local_width], head_full[:, 3 * local_width :]
    up_full, down_full = unit_full[:, :units_here], unit_full[:, units_here:]
    tokens_full = gather_cols(tokens)
    cot_full = gather_cols(cotangent)
    out_bias_full = lax.all_gather(out_bias, "mdl", axis=0, tiled=True).astype(f32)

    inside, segment = crop_layout(lengths, padding, row_len)
    crop_hot = inside[0].astype(bf16)
    crop_hot32 = inside[0].astype(f32)

    def spread(part):
        return exact_dot(crop_hot32, mod_full[:, part])

    head_tok = mm(crop_hot, head_mask[0].astype(bf16), ((1,), (0,)))
    head_units = jnp.repeat(head_tok, head_width, axis=1).astype(bf16)
    chan_tok = mm(crop_hot, chan_mask[0].astype(bf16), ((1,), (0,)))
    chan_units = jnp.repeat(chan_tok, units_here // groups_here, axis=1)
    keep_rows = keep_mask.astype(f32)[:, None]

    start_rows = tokens_full.astype(f32)
    normed_one, inverse_one = norm_rows(start_rows)
    modulated_one = (normed_one * (1.0 + spread(1)) + spread(0)).astype(bf16)
    projected = mm(modulated_one, qkv_full, ((1,), (0,)))
    qv_bias32 = qv_bias.astype(f32)
    queries = (projected[:, :local_width] + qv_bias32[0]).astype(bf16)
    key_rows = projected[:, local_width : 2 * local_width].astype(bf16)
    value_rows = (projected[:, 2 * local_width :] + qv_bias32[1]).astype(bf16)

    def heads(rows):
        return rows.reshape(row_len, heads_here, head_width)

    attend_now, logsum_rows = attend_row(
        heads(queries), heads(key_rows), heads(value_rows), segment[0], score_scale
    )
    attended = (attend_now.reshape(row_len, local_width) * head_units.astype(f32)).astype(bf16)
    branch_own = scatter_cols(mm(attended, out_full, ((1,), (1,))))
    attn_branch = gather_cols(branch_own).astype(f32) + out_bias_full
    gate_one = spread(2)
    middle = start_rows + gate_one * attn_branch
    normed_two, inverse_two = norm_rows(middle)
    scale_two = spread(4)
    modulated_two = (normed_two * (1.0 + scale_two) + spread(3)).astype(bf16)
    up_pre = mm(modulated_two, up_full, ((1,), (0,))) + up_bias.astype(f32)
    gelu_values, gelu_back = jax.vjp(lambda pre: jax.nn.gelu(pre, approximate=True), up_pre)
    hidden = (gelu_values * chan_units).astype(bf16)
    mlp_out = scatter_cols(mm(hidden, down_full, ((1,), (1,)))).astype(f32) + down_bias.astype(f32)
    gate_two = spread(5)
    output = (own_cols(middle) + own_cols(gate_two) * keep_rows * mlp_out).astype(bf16)

    grad_rows = cot_full.astype(f32)
    grad_mlp = (grad_rows * gate_two * keep_rows).astype(bf16)
    grad_hidden = mm(grad_mlp, down_full, ((1,), (0,)))
    grad_down = mm(grad_mlp, hidden, ((0,), (0,)))
    grad_down_bias = jnp.sum(own_cols(grad_mlp).astype(f32), axis=0)
    grad_up_pre = gelu_back(grad_hidden * chan_units)[0].astype(bf16)
    grad_up = mm(modulated_two, grad_up_pre, ((0,), (0,)))
    grad_up_bias = jnp.sum(grad_up_pre.astype(f32), axis=0)
    grad_units = lax.psum_scatter(
        jnp.concatenate([grad_up, grad_down], axis=1).astype(bf16), "tok", scatter_dimension=0, tiled=True
    ).astype(f32)
    two_own = scatter_cols(mm(grad_up_pre, up_full, ((1,), (1,))))
    grad_two = gather_cols(two_own).astype(f32)

    def norm_back(grad_norm, normed, inverse):
        return inverse * (
            grad_norm
            - jnp.mean(grad_norm, axis=1, keepdims=True)
            - normed * jnp.mean(grad_norm * normed, axis=1, keepdims=True)
        )

    grad_middle = grad_rows + norm_back(grad_two * (1.0 + scale_two), normed_two, inverse_two)
    grad_attn = (grad_middle * gate_one).astype(bf16)
    grad_out = mm(grad_attn, attended, ((0,), (0,)))
    grad_out_bias = jnp.sum(own_cols(grad_attn).astype(f32), axis=0)
    grad_att = mm(grad_attn, out_full, ((1,), (0,))).astype(bf16) * head_units
    query_grads, key_grads, value_grads = attend_back(
        heads(queries), heads(key_rows), heads(value_rows), segment[0], logsum_rows, heads(grad_att), score_scale
    )
    grad_qkv_rows = jnp.concatenate(
        [part.reshape(row_len, local_width).astype(bf16) for part in (query_grads, key_grads, value_grads)], axis=1
    )
    grad_qkv = mm(modulated_one, grad_qkv_rows, ((0,), (0,)))
    grad_bias_rows = jnp.sum(grad_qkv_rows.astype(f32), axis=0)
    grad_qv_bias = jnp.stack([grad_bias_rows[:local_width], grad_bias_rows[2 * local_width :]], axis=0)
    grad_heads = lax.psum_scatter(
        jnp.concatenate([grad_qkv, grad_out], axis=1).astype(bf16), "tok", scatter_dimension=0, tiled=True
    ).astype(f32)
    grad_one = scatter_cols(mm(grad_qkv_rows, qkv_full, ((1,), (1,)))).astype(f32)
    normed_one_own = own_cols(normed_one)
    grad_norm = grad_one * (1.0 + own_cols(spread(1)))
    totals = lax.psum(
        jnp.stack([jnp.sum(grad_norm, axis=1), jnp.sum(grad_norm * normed_one_own, axis=1)]), "mdl"
    )
    grad_middle_own = own_cols(grad_middle)
    grad_tokens = grad_middle_own + inverse_one * (
        grad_norm - totals[0][:, None] / full_width - normed_one_own * totals[1][:, None] / full_width
    )
    two_own32 = two_own.astype(f32)
    grad_per_token = jnp.concatenate(
        [
            grad_one,
            grad_one * normed_one_own,
            grad_middle_own * own_cols(attn_branch),
            two_own32,
            two_own32 * own_cols(normed_two),
            cotangent.astype(f32) * keep_rows * mlp_out,
        ],
        axis=1,
    )
    grad_mod_own = lax.dot_general(
        crop_hot32, grad_per_token, (((0,), (0,)), ((), ())), precision=lax.Precision.HIGHEST, preferred_element_type=f32
    )
    grad_mod = lax.all_gather(grad_mod_own, "tok", axis=0, tiled=True)
    grad_ada_bias = jnp.sum(grad_mod.reshape(all_crops, 6, local_width), axis=0)
    grad_ada = lax.dot_general(
        cond_own.astype(f32), grad_mod, (((0,), (0,)), ((), ())), precision=lax.Precision.HIGHEST, preferred_element_type=f32
    ).reshape(own_rows, 6, local_width)
    cond_part = lax.dot_general(
        grad_mod, ada_own.astype(f32), (((1,), (1,)), ((), ())), precision=lax.Precision.HIGHEST, preferred_element_type=f32
    )
    grad_cond = lax.all_gather(lax.psum(cond_part, "mdl"), "tok", axis=1, tiled=True)
    silu_values, silu_back = jax.vjp(jax.nn.silu, embedding)
    grad_embed = silu_back(own_cols(grad_cond))[0]
    freq_rows = time_weight.shape[0]
    own_feats = lax.dynamic_slice_in_dim(step_feats, tok_at * freq_rows, freq_rows, axis=1)
    grad_time = exact_dot(own_feats.T, grad_embed)
    grad_class = exact_dot(label_hot.astype(f32).T, grad_embed)
    grad_qv_bias, grad_out_bias, grad_up_bias, grad_down_bias = lax.psum(
        (grad_qv_bias, grad_out_bias, grad_up_bias, grad_down_bias), "tok"
    )
    return (
        output,
        grad_tokens,
        grad_heads[:, : 3 * local_width].reshape(own_rows, 3, local_width),
        grad_qv_bias,
        grad_heads[:, 3 * local_width :].T,
        grad_out_bias,
        grad_units[:, :units_here],
        grad_up_bias,
        grad_units[:, units_here:].T,
        grad_down_bias,
        grad_ada,
        grad_ada_bias,
        grad_time,
        grad_class,
    )


def solution(mesh):
    body = on_device if dict(mesh.shape) == {"tok": 8, "mdl": 4} else on_device_any
    return jax.shard_map(
        body,
        mesh=mesh,
        in_specs=(
            P("tok", "mdl"),
            P("tok", "mdl"),
            P("tok", None),
            P("tok", None),
            P("tok", None),
            P("tok", None),
            P("tok", None, "mdl"),
            P("tok", None, "mdl"),
            P("tok"),
            P("tok", None, "mdl"),
            P(None, "mdl"),
            P("mdl", "tok"),
            P("mdl"),
            P("tok", "mdl"),
            P("mdl"),
            P("mdl", "tok"),
            P("mdl"),
            P("tok", None, "mdl"),
            P(None, "mdl"),
            P("tok", "mdl"),
            P(None, "mdl"),
        ),
        out_specs=(
            P("tok", "mdl"),
            P("tok", "mdl"),
            P("tok", None, "mdl"),
            P(None, "mdl"),
            P("mdl", "tok"),
            P("mdl"),
            P("tok", "mdl"),
            P("mdl"),
            P("mdl", "tok"),
            P("mdl"),
            P("tok", None, "mdl"),
            P(None, "mdl"),
            P("tok", "mdl"),
            P(None, "mdl"),
        ),
        check_vma=False,
    )
```

profile of v0, /device:TPU:0, one launch (start us, length us, event | category | flops | bytes accessed | tf_op | source)
XLA Modules:
  0.0 325.0 jit_solution(10321214403949179064)
XLA Ops:
  0.6 0.7 convert_bitcast_fusion
  1.3 0.5 fusion.12
  1.8 0.8 copy.37
  2.6 0.8 copy.38
  3.4 0.7 pad_add_fusion.masks
  4.0 0.7 fusion.11
  4.8 0.6 bitcast_convert_fusion.bias_table
  5.4 0.1 multiply_cosine_fusion
  5.5 0.6 select_maximum_fusion.feats_own
  6.1 122.4 %shard_map.308 = (f32[8,8,640]{2,1,0:T(8,128)}, f32[64,288]{1,0:T(8,128)}, bf16[64,144]{1,0:T(8,128)(2,1)}, f32[1,1152]{1,0:T(1,128)}, bf16[6,32,1152]{2,1,0:T(8...) custom-call(f32[8,256]{1,0:T(8,128)} %select_maximum_fusion.feats_ow, ...), custom_call_target="tpu_custom_call" | custom-call | tf_op jit(solution)/shard_map/pallas_call | solution.py:736
  128.5 1.0 convert_reduce_fusion
  129.5 1.5 slice_bitcast_fusion
  131.0 0.6 convert_element_type.32
  131.6 54.9 %shard_map.309 = (bf16[4,1280,288]{2,1,0:T(8,128)(2,1)}, bf16[1280,1152]{1,0:T(8,128)(2,1)}, bf16[1152,2304]{1,0:T(8,128)(2,1)}, f32[1,1152]{1,0:T(1,128)}, f32[1,1152]{1,0:T(1,128)}) custom-call(bf16[1280,1152]{1,0:T(8,128)(2,1)} %get-tuple-element.58.branch_full, bf16[1280,1152]{1,0:T(8,128)(2,1)} %get-tuple-element.59.tokens_full, ...), custom_call_target="tpu_custom_call" | custom-call | tf_op jit(solution)/shard_map/pallas_call | solution.py:958
  186.6 122.8 %shard_map.310 = (bf16[288,1280]{1,0:T(8,128)(2,1)}, f32[288,1280]{1,0:T(8,128)}, f32[144,1152]{1,0:T(8,128)}, f32[144,1152]{1,0:T(8,128)}, f32[3,144,288]{2,1,0...) custom-call(bf16[1280,1152]{1,0:T(8,128)(2,1)} %get-tuple-element.68, ...), custom_call_target="tpu_custom_call" | custom-call | tf_op jit(solution)/shard_map/pallas_call | solution.py:1690
  309.4 2.0 fusion.5
  311.4 0.8 slice.24
  312.2 0.1 reshape.75
  312.3 0.7 fusion.14
  312.9 0.7 slice.34
  313.6 0.1 slice.25
  313.7 0.6 slice.32
  314.3 2.6 fusion.1
  316.9 2.1 copy.47
  319.0 1.1 copy.48
  320.1 0.8 copy.49
  321.0 0.0 copy-done.5
  321.0 0.7 copy.50
  321.7 0.8 copy.51
  322.5 0.8 copy.52
  323.4 1.1 copy.53
  324.4 0.6 copy.54
  (14 shorter events, 0.0 us)
Async XLA Ops:
  309.4 9.6 %copy-start = (f32[288,1280]{1,0:T(8,128)S(1)}, f32[288,1280]{1,0:T(8,128)}, u32[]{:S(2)}) copy-start(f32[288,1280]{1,0:T(8,128)} %get-tuple-element.92) | copy-start | bytes 4423684
  316.9 3.2 copy-start.4
  319.0 2.0 copy-start.5
  319.0 2.6 copy-start.3
  320.1 2.4 copy-start.2
  320.1 3.2 copy-start.1
  322.5 1.9 copy-start.6
where the time goes:
time: 326 us; the launch traced here: 325 us
  Pallas kernels  300 us (92%)
  local copies, waits for them, and re-layouts  14.6 us (4%)
  other arithmetic  4.95 us (2%)
  matrix products  4.61 us (1%)
    pallas_call x1, Pallas kernels, rear(): pl.pallas_call(rear_kernel, out_shape=(shape((local_width, rows), bf16),...  123 us
    pallas_call x1, Pallas kernels, front(): pl.pallas_call(front_kernel, out_shape=(shape((tok_count, slots, small_wi...  122 us
    pallas_call x1, Pallas kernels, feed(): pl.pallas_call(feed_kernel, out_shape=(jax.ShapeDtypeStruct((4, rows, loc...  54.9 us
    unnamed x24, local copies, waits for them, and re-layouts  9.62 us

commit v1 on v0

--- a/solution.py
+++ b/solution.py
@@ -350,22 +350,31 @@
     seg_row,
     unit_full,
     cot_blocks,
+    tokens_full_out,
+    qkv_full_out,
+    out_full_out,
+    mod_one_out,
+    stats,
+    q_out,
+    k_out,
+    v_out,
+    logsum,
+    attended,
+    branch_full,
+    tokens_out,
+    cotangent_out,
+    out_row,
+    up_row,
+    down_row,
+    tokens,
+    cotangent,
     tokens_full,
+    mod_one,
     qkv_full,
     out_full,
-    mod_one,
-    stats,
     q_heads,
     k_heads,
     v_heads,
-    logsum,
-    attended,
-    branch_full,
-    tokens,
-    cotangent,
-    out_row,
-    up_row,
-    down_row,
     small_own,
     head_shard,
     unit_shard,
@@ -407,6 +416,7 @@
     sum_sends,
     sum_recvs,
     own_sems,
+    store_sems,
 ):
     tok_at = lax.axis_index("tok")
     mdl_at = lax.axis_index("mdl")
@@ -481,6 +491,24 @@
     head_line.start()
     tokens[...] = token_flip[...].T
     cotangent[...] = cot_flip[...].T
+    stores = [
+        pltpu.make_async_copy(source, target, store_sems.at[index])
+        for index, (source, target) in enumerate(
+            (
+                (tokens, tokens_out),
+                (cotangent, cotangent_out),
+                (tokens_full, tokens_full_out),
+                (mod_one, mod_one_out),
+                (qkv_full, qkv_full_out),
+                (out_full, out_full_out),
+                (q_heads, q_out),
+                (k_heads, k_out),
+                (v_heads, v_out),
+            )
+        )
+    ]
+    stores[0].start()
+    stores[1].start()
     token_quad.start((0, 1))
     own_copies = (
         pltpu.make_async_copy(head_shard, head_line.slot(tok_at), own_sems.at[0]),
@@ -615,16 +643,12 @@
     late_mods.start(lambda other: late_out.at[mdl_at], late_out)
     for chunk in range(chunks):
         token_quad.arrive_rest(chunk)
-    own_copies[0].wait()
     own_copies[2].wait()
-    head_line.arrive_across()
-    qkv_full[...] = head_full[:, : 3 * local_width]
-    out_full[...] = head_full[:, 3 * local_width :]
 
     def span(chunk):
         return pl.ds(pl.multiple_of(chunk * size, 128), size)
 
-    def project(chunk, carry):
+    def modulate(chunk, carry):
         here = span(chunk)
         joined = jnp.concatenate([token_blocks[at, here, :] for at in range(4)], axis=1)
         tokens_full[here, :] = joined
@@ -635,6 +659,20 @@
         stats[here, 1:2] = inverse
         scale = mm(hot_now, pieces[1], ((1,), (0,)))
         mod_one[here, :] = (normed * (1.0 + scale) + mm(hot_now, pieces[0], ((1,), (0,)))).astype(bf16)
+        return carry
+
+    lax.fori_loop(0, chunks, modulate, 0)
+    stores[2].start()
+    stores[3].start()
+    own_copies[0].wait()
+    head_line.arrive_across()
+    qkv_full[...] = head_full[:, : 3 * local_width]
+    out_full[...] = head_full[:, 3 * local_width :]
+    stores[4].start()
+    stores[5].start()
+
+    def project(chunk, carry):
+        here = span(chunk)
         projected = (mm(mod_one[here, :], qkv_full[...], ((1,), (0,))) + qkv_bias).astype(bf16)
         for head in range(heads):
             for kind, ref in enumerate((q_heads, k_heads, v_heads)):
@@ -644,6 +682,8 @@
         return carry
 
     lax.fori_loop(0, chunks, project, 0)
+    for copy in stores[6:]:
+        copy.start()
     for head in range(heads):
         v_flip[head] = v_heads[head].T
 
@@ -708,6 +748,8 @@
         branch.wait_send(chunk)
     own_copies[1].wait()
     own_copies[3].wait()
+    for copy in stores:
+        copy.wait()
 
 
 def front(
@@ -767,8 +809,17 @@
             shape((1, local_width), f32),
         ),
         in_specs=[vmem] * 13 + [scalar] * 3 + [vmem] * 2,
-        out_specs=(vmem,) * 11 + (anywhere,) * 2 + (vmem,) * 16,
+        out_specs=(vmem,) * 11 + (anywhere,) * 6 + (vmem,) + (anywhere,) * 3 + (vmem,) * 3 + (anywhere,) * 2 + (vmem,) * 3,
         scratch_shapes=[
+            low(rows, local_width),
+            low(rows, local_width),
+            low(rows, whole),
+            low(rows, whole),
+            low(whole, 3 * local_width),
+            low(whole, local_width),
+            low(heads, rows, head_width),
+            low(heads, rows, head_width),
+            low(heads, rows, head_width),
             pltpu.VMEM((slots, small_width), f32),
             low(own_rows, head_width_all),
             low(own_rows, unit_width),
@@ -810,6 +861,7 @@
             dma((3, chunks)),
             dma((3, chunks)),
             dma((4,)),
+            dma((9,)),
         ],
         compiler_params=pltpu.CompilerParams(collective_id=0, has_side_effects=True, vmem_limit_bytes=63 * 2**20),
     )(
@@ -1206,6 +1258,7 @@
     ada_parts,
     cond_own,
     embedding,
+    small_all,
     output,
     grad_flip,
     up_out,
@@ -1215,7 +1268,8 @@
     gmod_sum,
     grad_ada,
     ada_bias_grad,
-    grad_embed,
+    grad_time,
+    class_flip,
     head_grads,
     gmod_all,
     token_buf,
@@ -1305,8 +1359,7 @@
 
     def mod_load(index):
         at = pl.ds(pl.multiple_of(index * third, 128), third)
-        slot = lax.rem(index, 2)
-        return pltpu.make_async_copy(mod_any.at[:, at], mod_buf.at[slot], mod_sems.at[slot])
+        return pltpu.make_async_copy(mod_any.at[:, at], mod_buf, mod_sems.at[0])
 
     fetches = [
         pltpu.make_async_copy(source, target, fetch_sems.at[index])
@@ -1349,7 +1402,6 @@
     for copy in fetches[3:]:
         copy.start()
     mod_load(0).start()
-    mod_load(1).start()
     attn_sums[...] = jnp.zeros_like(attn_sums)
     out_sum[...] = jnp.zeros_like(out_sum)
     for copy in fetches[:3]:
@@ -1501,9 +1553,9 @@
     def grads(index, carry):
         at = pl.ds(pl.multiple_of(index * third, 128), third)
         mod_load(index).wait()
-        weight = mm(mod_buf[lax.rem(index, 2)], qkv_rows[...], ((0,), (0,))).astype(bf16)
+        weight = mm(mod_buf[...], qkv_rows[...], ((0,), (0,))).astype(bf16)
         full_grads[at, :] = jnp.concatenate([weight, out_sum[at, :].astype(bf16)], axis=1)
-        pl.when(index == 0)(lambda: mod_load(2).start())
+        pl.when(index < 2)(lambda: mod_load(index + 1).start())
         line.serve(served + index)
         return carry
 
@@ -1649,7 +1701,25 @@
     grad_cond = jnp.concatenate([cond_slots[0], cond_slots[1]], axis=1)
     embed = embedding[...]
     gate = 1.0 / (1.0 + jnp.exp(-embed))
-    grad_embed[...] = grad_cond * gate * (1.0 + embed * (1.0 - gate))
+    grad_embed = grad_cond * gate * (1.0 + embed * (1.0 - gate))
+    freq_count, class_count = grad_time.shape[0] * tok_count, class_flip.shape[1]
+    crops = tok_count * slots
+    embed_high, embed_rest = split_two(grad_embed)
+    feats = small_all[:, :, :freq_count].reshape(crops, freq_count)
+    freq_rows = grad_time.shape[0]
+    freq_at = lax.broadcasted_iota(jnp.int32, (freq_count, freq_rows), 0)
+    own_freq = lax.broadcasted_iota(jnp.int32, (freq_count, freq_rows), 1) + tok_at * freq_rows
+    pick_own = jnp.where(freq_at == own_freq, 1.0, 0.0).astype(bf16)
+    total = jnp.zeros(grad_time.shape, f32)
+    for values in split_three(feats):
+        own_feats = mm(values, pick_own, ((1,), (0,))).astype(bf16)
+        total = total + mm(own_feats, embed_high, ((0,), (0,))) + mm(own_feats, embed_rest, ((0,), (0,)))
+    grad_time[...] = total
+    label_col = small_all[:, :, freq_count + local_width :].reshape(crops, small_all.shape[2] - freq_count - local_width)[:, 0:1]
+    crop_at = lax.broadcasted_iota(jnp.int32, (crops, class_count), 0)
+    class_at = lax.broadcasted_iota(jnp.int32, (crops, class_count), 1).astype(f32)
+    chosen = jnp.where((lax.rem(crop_at, slots) < slots - 2) & (class_at == label_col), 1.0, 0.0).astype(bf16)
+    class_flip[...] = mm(embed_high, chosen, ((0,), (0,))) + mm(embed_rest, chosen, ((0,), (0,)))
     gmods.wait_send(lambda other: gmod_low.at[tok_at], gmod_low)
     row_peers.wait_send(lambda other: row_sums.at[mdl_at], row_sums)
     pl.when(mdl_at != owner)(lambda: part_copy(mdl_at).wait_send())
@@ -1667,7 +1737,7 @@
 def rear(
     two_full, branch_full, tokens_full, cot_blocks, mlp_blocks, unit_grads, q_heads, k_heads, v_heads, mod_one, qkv_full, out_full, attended,
     hot, hot_keep, pieces, own_pieces, out_bias_full, out_bias, down_bias, head_rows, logsum, seg_row, tokens, cotangent, stats_one,
-    up_bias_sum, mlp_sum, ada_parts, cond_own, embedding, tok_count,
+    up_bias_sum, mlp_sum, ada_parts, cond_own, embedding, small_all, freq_rows, class_count, tok_count,
 ):
     rows, local_width = tokens.shape
     width, three = qkv_full.shape
@@ -1699,10 +1769,11 @@
             shape((slots, mod_width), f32),
             shape((6, own_rows, local_width), f32),
             shape((6, local_width), f32),
-            shape(embedding.shape, f32),
+            shape((freq_rows, local_width), f32),
+            shape((local_width, class_count), f32),
         ),
-        in_specs=[anywhere] * 13 + [vmem] * 18,
-        out_specs=(vmem,) * 10,
+        in_specs=[anywhere] * 13 + [vmem] * 19,
+        out_specs=(vmem,) * 11,
         scratch_shapes=[
             wide(own_rows, total),
             wide(tok_count, slots, mod_width),
@@ -1713,7 +1784,7 @@
             low(heads, rows, head_width),
             low(heads, rows, head_width),
             low(heads, rows, head_width),
-            low(2, rows, width // 3),
+            low(rows, width // 3),
             low(width, three),
             low(width, local_width),
             low(rows, local_width),
@@ -1767,8 +1838,35 @@
     )(
         two_full, branch_full, tokens_full, cot_blocks, mlp_blocks, unit_grads, q_heads, k_heads, v_heads, mod_one, qkv_full, out_full, attended,
         hot, hot_keep, pieces, own_pieces, out_bias_full, out_bias, down_bias, head_rows, logsum, seg_row, tokens, cotangent, stats_one,
-        up_bias_sum, mlp_sum, ada_parts, cond_own, embedding,
-    )
+        up_bias_sum, mlp_sum, ada_parts, cond_own, embedding, small_all,
+    )
+
+
+def deliver_kernel(*refs):
+    count = (len(refs) - 1) // 3
+    sources, targets, rooms, sems = refs[:count], refs[count : 2 * count], refs[2 * count : 3 * count], refs[3 * count]
+    loads = [pltpu.make_async_copy(sources[at], rooms[at], sems.at[0, at]) for at in range(count)]
+    stores = [pltpu.make_async_copy(rooms[at], targets[at], sems.at[1, at]) for at in range(count)]
+    for copy in loads:
+        copy.start()
+    for load, store in zip(loads, stores):
+        load.wait()
+        store.start()
+    for copy in stores:
+        copy.wait()
+
+
+def deliver(arrays):
+    anywhere = pl.BlockSpec(memory_space=pl.ANY)
+    return pl.pallas_call(
+        deliver_kernel,
+        out_shape=tuple(jax.ShapeDtypeStruct(array.shape, array.dtype) for array in arrays),
+        in_specs=[anywhere] * len(arrays),
+        out_specs=(anywhere,) * len(arrays),
+        scratch_shapes=[pltpu.VMEM(array.shape, array.dtype) for array in arrays]
+        + [pltpu.SemaphoreType.DMA((2, len(arrays)))],
+        compiler_params=pltpu.CompilerParams(vmem_limit_bytes=67043328),
+    )(*arrays)
 
 
 def on_device(
@@ -1858,27 +1956,23 @@
         out_weight.T, up_weight, down_weight.T, tokens.T, cotangent.T, lengths, padding, labels, masks,
         keep_mask.reshape(-1, lanes), heads_here, tok_count,
     )
-    all_crops = tok_count * slots
-    real_crop = (jnp.arange(all_crops, dtype=jnp.int32) % slots < slot_count)[:, None]
-    step_feats = small_all[:, :, :freq_count].reshape(all_crops, freq_count)
-    label_all = small_all[:, :, freq_count + local_width].reshape(all_crops).astype(jnp.int32)
-    label_hot = ((label_all[:, None] == jnp.arange(class_table.shape[0], dtype=jnp.int32)[None, :]) & real_crop).astype(f32)
     mlp_blocks, two_low, unit_grads, grad_up_bias, mlp_sums = feed(
         branch_low, tokens_full, cot_blocks, hot, hot_keep, pieces, out_bias_full, unit_full, up_row, chan_rows
     )
-    output, grad_tokens, grad_up, grad_down, grad_qkv, grad_out, gmod_sum, grad_ada, grad_ada_bias, grad_embed = rear(
+    output, grad_tokens, grad_up, grad_down, grad_qkv, grad_out, gmod_sum, grad_ada, grad_ada_bias, grad_time, grad_class = rear(
         two_low, branch_low, tokens_full, cot_blocks, mlp_blocks, unit_grads, q_heads, k_heads, v_heads, modulated_one, qkv_full, out_full,
         attended, hot, hot_keep, pieces, own_pieces, out_bias_full, out_row, down_row, head_rows,
-        logsum_rows, seg_row, tokens_own, cot_own, stats_one, grad_up_bias, mlp_sums, ada_parts, cond_own, embedding, tok_count,
+        logsum_rows, seg_row, tokens_own, cot_own, stats_one, grad_up_bias, mlp_sums, ada_parts, cond_own, embedding,
+        small_all, freq_rows, class_table.shape[0], tok_count,
+    )
+    output, grad_tokens, grad_up, grad_down, grad_qkv, grad_out, grad_ada, grad_ada_bias, grad_time, grad_class = deliver(
+        (output, grad_tokens, grad_up, grad_down, grad_qkv, grad_out, grad_ada, grad_ada_bias, grad_time, grad_class)
     )
     bias_total = gmod_sum[slot_count:].reshape(-1)
     grad_qv_bias = bias_total[: 2 * local_width].reshape(2, local_width)
     grad_out_bias = bias_total[2 * local_width : 3 * local_width]
     grad_up_bias = bias_total[3 * local_width : 3 * local_width + units_here]
     grad_down_bias = bias_total[3 * local_width + units_here : 4 * local_width + units_here]
-    own_feats = lax.dynamic_slice_in_dim(step_feats, tok_at * freq_rows, freq_rows, axis=1)
-    grad_time = exact_dot(own_feats.T, grad_embed)
-    grad_class = exact_dot(label_hot.T, grad_embed)
     return (
         output.T,
         grad_tokens.T,
@@ -1893,7 +1987,7 @@
         jnp.transpose(grad_ada, (1, 0, 2)),
         grad_ada_bias,
         grad_time,
-        grad_class,
+        grad_class.T,
     )
 
 

time: 326 us -> 312 us (0.957)
  local copies, waits for them, and re-layouts: 14.6 us -> 4.44 us
  matrix products: 4.61 us -> 0 us
    unnamed x24 -> x2, local copies, waits for them, and re-layouts: 9.62 us -> 1.54 us
    pallas_call x0 -> x1, Pallas kernels: none -> 5.82 us  [deliver(): pl.pallas_call(deliver_kernel, out_shape=tuple((jax.ShapeDtypeStruct(arra...]
    dot_general x2 -> x0, matrix products: 4.61 us -> none  [exact_dot(): jnp.dot(left, right, precision=lax.Precision.HIGHEST, preferred_element_t...]
    pallas_call x1, Pallas kernels: 122 us -> 118 us  [front(): pl.pallas_call(front_kernel, out_shape=(shape((tok_count, slots, small_wi...]
where the time goes in v1:
time: 312 us; the launch traced here: 311 us
  Pallas kernels  303 us (97%)
  local copies, waits for them, and re-layouts  4.44 us (1%)
  other arithmetic  3.39 us (1%)
    pallas_call x1, Pallas kernels, rear(): pl.pallas_call(rear_kernel, out_shape=(shape((local_width, rows), bf16),...  124 us
    pallas_call x1, Pallas kernels, front(): pl.pallas_call(front_kernel, out_shape=(shape((tok_count, slots, small_wi...  118 us
    pallas_call x1, Pallas kernels, feed(): pl.pallas_call(feed_kernel, out_shape=(jax.ShapeDtypeStruct((4, rows, loc...  54.9 us

profile of v1, /device:TPU:0, one launch (start us, length us, event | category | flops | bytes accessed | tf_op | source)
XLA Modules:
  0.0 311.3 jit_solution(8490270693697214522)
XLA Ops:
  0.6 0.7 convert_bitcast_fusion
  1.3 0.8 copy.35
  2.1 0.8 copy.36
  2.9 0.7 pad_add_fusion.masks
  3.5 0.7 fusion.4
  4.2 0.6 bitcast_convert_fusion.bias_table
  4.9 0.1 multiply_cosine_fusion
  5.0 0.6 select_maximum_fusion.feats_own
  5.6 118.1 %shard_map.308 = (f32[8,8,640]{2,1,0:T(8,128)}, f32[64,288]{1,0:T(8,128)}, bf16[64,144]{1,0:T(8,128)(2,1)}, f32[1,1152]{1,0:T(1,128)}, bf16[6,32,1152]{2,1,0:T(8...) custom-call(f32[8,256]{1,0:T(8,128)} %select_maximum_fusion.feats_ow, ...), custom_call_target="tpu_custom_call" | custom-call | tf_op jit(solution)/shard_map/pallas_call | solution.py:778
  123.7 54.9 %shard_map.309 = (bf16[4,1280,288]{2,1,0:T(8,128)(2,1)}, bf16[1280,1152]{1,0:T(8,128)(2,1)}, bf16[1152,2304]{1,0:T(8,128)(2,1)}, f32[1,1152]{1,0:T(1,128)}, f32[1,1152]{1,0:T(1,128)}) custom-call(bf16[1280,1152]{1,0:T(8,128)(2,1)} %get-tuple-element.69.branch_full, bf16[1280,1152]{1,0:T(8,128)(2,1)} %get-tuple-element.70.tokens_full, ...), custom_call_target="tpu_custom_call" | custom-call | tf_op jit(solution)/shard_map/pallas_call | solution.py:1010
  178.6 123.9 %shard_map.310 = (bf16[288,1280]{1,0:T(8,128)(2,1)}, f32[288,1280]{1,0:T(8,128)}, f32[144,1152]{1,0:T(8,128)}, f32[144,1152]{1,0:T(8,128)}, f32[3,144,288]{2,1,0...) custom-call(bf16[1280,1152]{1,0:T(8,128)(2,1)} %get-tuple-element.79, ...), custom_call_target="tpu_custom_call" | custom-call | tf_op jit(solution)/shard_map/pallas_call | solution.py:1760
  302.5 5.8 %shard_map.311 = (bf16[288,1280]{1,0:T(8,128)(2,1)}, f32[288,1280]{1,0:T(8,128)}, f32[144,1152]{1,0:T(8,128)}, f32[144,1152]{1,0:T(8,128)}, f32[3,144,288]{2,1,0...) custom-call(bf16[288,1280]{1,0:T(8,128)(2,1)} %get-tuple-element.103, ...), custom_call_target="tpu_custom_call" | custom-call | tf_op jit(solution)/shard_map/pallas_call | solution.py:1861
  308.4 0.8 slice.18
  309.2 0.1 reshape.56
  309.3 0.7 fusion.5
  309.9 0.7 slice.26
  310.6 0.1 slice.19
  310.7 0.6 slice.24
  (1 shorter events, 0.0 us)

commit v2 on v1

--- a/solution.py
+++ b/solution.py
@@ -871,23 +871,26 @@
 
 
 def feed_kernel(
-    branch_full,
+    branch_any,
     tokens_full,
     cot_blocks,
+    unit_any,
     hot,
     hot_keep,
     pieces,
     out_bias,
-    unit_full,
     up_bias,
     chan_rows,
     mlp_part,
     two_full,
-    unit_grads,
+    grads_any,
     up_bias_grad,
     mlp_sums,
     token_buf,
     cot_buf,
+    branch_buf,
+    unit_full,
+    unit_grads,
     mod_rows,
     gup_rows,
     hid_rows,
@@ -901,6 +904,8 @@
     recvs,
     load_sems,
     store_sems,
+    unit_sems,
+    grad_sems,
 ):
     mdl_at = lax.axis_index("mdl")
     rows, width = two_full.shape
@@ -908,7 +913,6 @@
     size = rows // chunks
     units = up_bias.shape[1]
     local_width = cot_blocks.shape[2]
-    greet_quad(mdl_at)
     twos = RowReduce(mdl_at, two_part, near_in, own_sum, far_in, two_full, sends, recvs)
 
     def span(chunk):
@@ -918,6 +922,7 @@
         return (
             pltpu.make_async_copy(tokens_full.at[span(chunk), :], token_buf.at[slot], load_sems.at[0, slot]),
             pltpu.make_async_copy(cot_blocks.at[:, span(chunk), :], cot_buf.at[slot], load_sems.at[1, slot]),
+            pltpu.make_async_copy(branch_any.at[span(chunk), :], branch_buf.at[slot], load_sems.at[2, slot]),
         )
 
     def store(chunk, slot):
@@ -925,6 +930,13 @@
 
     for copy in loads(0, 0):
         copy.start()
+    unit_loads = [
+        pltpu.make_async_copy(unit_any.at[:, pl.ds(part * units, units)], unit_full.at[:, pl.ds(part * units, units)], unit_sems.at[part])
+        for part in range(2)
+    ]
+    for copy in unit_loads:
+        copy.start()
+    greet_quad(mdl_at)
     up_bias_grad[...] = jnp.zeros_like(up_bias_grad)
     mlp_sums[...] = jnp.zeros_like(mlp_sums)
 
@@ -945,9 +957,10 @@
             return mm(hot_now, pieces[part], ((1,), (0,)))
 
         token_rows = token_buf[slot].astype(f32)
-        middle = token_rows + spread(2) * (branch_full[here, :].astype(f32) + out_bias[...])
+        middle = token_rows + spread(2) * (branch_buf[slot].astype(f32) + out_bias[...])
         normed, inverse = centre(middle)
         mod_rows[here, :] = (normed * (1.0 + spread(4)) + spread(3)).astype(bf16)
+        pl.when(chunk == 0)(lambda: unit_loads[0].wait())
         up_pre = mm(mod_rows[here, :], unit_full[:, :units], ((1,), (0,))) + up_bias[...]
         bend = math.sqrt(2.0 / math.pi)
         square = up_pre * up_pre
@@ -960,6 +973,7 @@
         def _():
             store(chunk - 2, slot).wait()
 
+        pl.when(chunk == 0)(lambda: unit_loads[1].wait())
         mlp_rows = mm(hid_rows[here, :], unit_full[:, units:], ((1,), (1,))).astype(bf16)
         for at in range(4):
             mlp_buf[slot, at] = mlp_rows[:, at * local_width : (at + 1) * local_width]
@@ -981,10 +995,15 @@
     twos.second(chunks - 1)
     third = width // 3
 
+    def grad_store(index):
+        at = pl.ds(pl.multiple_of(index * third, 128), third)
+        return pltpu.make_async_copy(unit_grads.at[at, :], grads_any.at[at, :], grad_sems.at[index])
+
     def grads(index, carry):
         at = pl.ds(pl.multiple_of(index * third, 128), third)
         unit_grads[at, :units] = mm(mod_rows[:, at], gup_rows[...], ((0,), (0,))).astype(bf16)
         unit_grads[at, units:] = mm(gmlp_rows[:, at], hid_rows[...], ((0,), (0,))).astype(bf16)
+        grad_store(index).start()
         pl.when(index == 1)(lambda: twos.third(chunks - 2))
         return carry
 
@@ -993,6 +1012,8 @@
     for chunk in range(chunks):
         twos.fourth(chunk)
         twos.wait_send(chunk)
+    for index in range(3):
+        grad_store(index).wait()
     store(chunks - 2, (chunks - 2) % 2).wait()
     store(chunks - 1, (chunks - 1) % 2).wait()
 
@@ -1016,11 +1037,14 @@
             jax.ShapeDtypeStruct((1, units), f32),
             jax.ShapeDtypeStruct((1, width), f32),
         ),
-        in_specs=[vmem, anywhere, anywhere] + [vmem] * 7,
-        out_specs=(anywhere, vmem, vmem, vmem, vmem),
+        in_specs=[anywhere] * 4 + [vmem] * 6,
+        out_specs=(anywhere, vmem, anywhere, vmem, vmem),
         scratch_shapes=[
             low(2, size, width),
             low(2, 4, size, local_width),
+            low(2, size, width),
+            low(width, 2 * units),
+            low(width, 2 * units),
             low(rows, width),
             low(rows, units),
             low(rows, units),
@@ -1032,11 +1056,13 @@
             low(chunks, size // 2, width),
             dma((3, chunks)),
             dma((3, chunks)),
-            dma((2, 2)),
+            dma((3, 2)),
             dma((2,)),
+            dma((2,)),
+            dma((3,)),
         ],
         compiler_params=pltpu.CompilerParams(collective_id=2, has_side_effects=True, vmem_limit_bytes=63 * 2**20),
-    )(branch_full, tokens_full, cot_blocks, hot, hot_keep, pieces, out_bias, unit_full, up_bias, chan_rows)
+    )(branch_full, tokens_full, cot_blocks, unit_full, hot, hot_keep, pieces, out_bias, up_bias, chan_rows)
 
 
 class ColumnReduce:
@@ -1098,7 +1124,7 @@
         self.line = lax.div(tok_at, 2)
         self.side = lax.rem(tok_at, 2)
         self.count = 4 * self.pieces
-        self.lag = 4
+        self.lag = 2
 
     def at(self, step):
         turn = lax.rem(step, 4)

time: 312 us -> 305 us (0.978)
  Pallas kernels: 303 us -> 296 us
    pallas_call x1, Pallas kernels: 54.9 us -> 50 us  [feed(): pl.pallas_call(feed_kernel, out_shape=(jax.ShapeDtypeStruct((4, rows, loc...]
where the time goes in v2:
time: 305 us; the launch traced here: 304 us
  Pallas kernels  296 us (97%)
  local copies, waits for them, and re-layouts  4.44 us (1%)
  other arithmetic  3.39 us (1%)
    pallas_call x1, Pallas kernels, rear(): pl.pallas_call(rear_kernel, out_shape=(shape((local_width, rows), bf16),...  122 us
    pallas_call x1, Pallas kernels, front(): pl.pallas_call(front_kernel, out_shape=(shape((tok_count, slots, small_wi...  118 us
    pallas_call x1, Pallas kernels, feed(): pl.pallas_call(feed_kernel, out_shape=(jax.ShapeDtypeStruct((4, rows, loc...  50 us

profile of v2, /device:TPU:0, one launch (start us, length us, event | category | flops | bytes accessed | tf_op | source)
XLA Modules:
  0.0 304.5 jit_solution(14237033221559057373)
XLA Ops:
  0.6 0.7 convert_bitcast_fusion
  1.3 0.8 copy.35
  2.1 0.8 copy.36
  2.9 0.7 pad_add_fusion.masks
  3.5 0.7 fusion.4
  4.2 0.6 bitcast_convert_fusion.bias_table
  4.9 0.1 multiply_cosine_fusion
  5.0 0.6 select_maximum_fusion.feats_own
  5.6 118.1 %shard_map.308 = (f32[8,8,640]{2,1,0:T(8,128)}, f32[64,288]{1,0:T(8,128)}, bf16[64,144]{1,0:T(8,128)(2,1)}, f32[1,1152]{1,0:T(1,128)}, bf16[6,32,1152]{2,1,0:T(8...) custom-call(f32[8,256]{1,0:T(8,128)} %select_maximum_fusion.feats_ow, ...), custom_call_target="tpu_custom_call" | custom-call | tf_op jit(solution)/shard_map/pallas_call | solution.py:778
  123.7 50.0 %shard_map.309 = (bf16[4,1280,288]{2,1,0:T(8,128)(2,1)}, bf16[1280,1152]{1,0:T(8,128)(2,1)}, bf16[1152,2304]{1,0:T(8,128)(2,1)}, f32[1,1152]{1,0:T(1,128)}, f32[1,1152]{1,0:T(1,128)}) custom-call(bf16[1280,1152]{1,0:T(8,128)(2,1)} %get-tuple-element.69.branch_any.branch_full, bf16[1280,1152]{1,0:T(8,128)(2,1)} %get-tuple-element.70.tokens_full, ...), custom_call_target="tpu_custom_call" | custom-call | tf_op jit(solution)/shard_map/pallas_call | solution.py:1031
  173.7 122.0 %shard_map.310 = (bf16[288,1280]{1,0:T(8,128)(2,1)}, f32[288,1280]{1,0:T(8,128)}, f32[144,1152]{1,0:T(8,128)}, f32[144,1152]{1,0:T(8,128)}, f32[3,144,288]{2,1,0...) custom-call(bf16[1280,1152]{1,0:T(8,128)(2,1)} %get-tuple-element.79, ...), custom_call_target="tpu_custom_call" | custom-call | tf_op jit(solution)/shard_map/pallas_call | solution.py:1786
  295.7 5.8 %shard_map.311 = (bf16[288,1280]{1,0:T(8,128)(2,1)}, f32[288,1280]{1,0:T(8,128)}, f32[144,1152]{1,0:T(8,128)}, f32[144,1152]{1,0:T(8,128)}, f32[3,144,288]{2,1,0...) custom-call(bf16[288,1280]{1,0:T(8,128)(2,1)} %get-tuple-element.103, ...), custom_call_target="tpu_custom_call" | custom-call | tf_op jit(solution)/shard_map/pallas_call | solution.py:1887
  301.5 0.8 slice.18
  302.4 0.1 reshape.56
  302.5 0.7 fusion.5
  303.1 0.7 slice.26
  303.8 0.1 slice.19
  303.9 0.6 slice.24
  (1 shorter events, 0.0 us)

commit v3 on v2

--- a/solution.py
+++ b/solution.py
@@ -1546,7 +1546,9 @@
     own_block(mdl_at, attn_sums[...], local_width, keep_sum(slots - 2, 2 * local_width))
     own_block(mdl_at, mlp_sum[...], local_width, keep_sum(slots - 1, units - split))
 
-    def gather_rows(chunk, carry):
+    pl.semaphore_wait(free_sem, 2)
+
+    def ones_step(chunk, carry):
         here = span(chunk)
         joined = jnp.concatenate(
             [part[head, here, :] for part in (q_heads, k_heads, v_heads) for head in range(heads)], axis=1
@@ -1555,15 +1557,6 @@
         total = jnp.sum(joined.astype(f32), axis=0, keepdims=True)
         gmod_own[slots - 2 : slots - 1, :local_width] += total[:, :local_width]
         gmod_own[slots - 2 : slots - 1, local_width : 2 * local_width] += total[:, 2 * local_width :]
-        return carry
-
-    lax.fori_loop(0, chunks, gather_rows, 0)
-    line.serve_range(served, served + 2)
-    served += 2
-    pl.semaphore_wait(free_sem, 2)
-
-    def ones_step(chunk, carry):
-        here = span(chunk)
         part = mm(qkv_rows[here, :], qkv_full[...], ((1,), (1,))).astype(bf16)
         for at in range(4):
             col_blocks[at, here, :] = part[:, at * local_width : (at + 1) * local_width]
@@ -1574,6 +1567,8 @@
 
     lax.fori_loop(0, chunks, ones_step, 0)
     ones.second(chunks - 1)
+    served += 2
+    line.serve_range(served, served + 2)
     served += 2
 
     def grads(index, carry):

time: 305 us -> 304 us (level)
  no operation moved by 1% of the time
where the time goes in v3:
time: 304 us; the launch traced here: 303 us
  Pallas kernels  294 us (97%)
  local copies, waits for them, and re-layouts  4.44 us (1%)
  other arithmetic  3.39 us (1%)
    pallas_call x1, Pallas kernels, rear(): pl.pallas_call(rear_kernel, out_shape=(shape((local_width, rows), bf16),...  120 us
    pallas_call x1, Pallas kernels, front(): pl.pallas_call(front_kernel, out_shape=(shape((tok_count, slots, small_wi...  118 us
    pallas_call x1, Pallas kernels, feed(): pl.pallas_call(feed_kernel, out_shape=(jax.ShapeDtypeStruct((4, rows, loc...  50 us

profile of v3, /device:TPU:0, one launch (start us, length us, event | category | flops | bytes accessed | tf_op | source)
XLA Modules:
  0.0 302.8 jit_solution(13634933095690143995)
XLA Ops:
  0.6 0.7 convert_bitcast_fusion
  1.3 0.8 copy.35
  2.1 0.8 copy.36
  2.9 0.7 pad_add_fusion.masks
  3.5 0.7 fusion.4
  4.2 0.6 bitcast_convert_fusion.bias_table
  4.9 0.1 multiply_cosine_fusion
  5.0 0.6 select_maximum_fusion.feats_own
  5.6 118.1 %shard_map.308 = (f32[8,8,640]{2,1,0:T(8,128)}, f32[64,288]{1,0:T(8,128)}, bf16[64,144]{1,0:T(8,128)(2,1)}, f32[1,1152]{1,0:T(1,128)}, bf16[6,32,1152]{2,1,0:T(8...) custom-call(f32[8,256]{1,0:T(8,128)} %select_maximum_fusion.feats_ow, ...), custom_call_target="tpu_custom_call" | custom-call | tf_op jit(solution)/shard_map/pallas_call | solution.py:778
  123.7 50.0 %shard_map.309 = (bf16[4,1280,288]{2,1,0:T(8,128)(2,1)}, bf16[1280,1152]{1,0:T(8,128)(2,1)}, bf16[1152,2304]{1,0:T(8,128)(2,1)}, f32[1,1152]{1,0:T(1,128)}, f32[1,1152]{1,0:T(1,128)}) custom-call(bf16[1280,1152]{1,0:T(8,128)(2,1)} %get-tuple-element.69.branch_any.branch_full, bf16[1280,1152]{1,0:T(8,128)(2,1)} %get-tuple-element.70.tokens_full, ...), custom_call_target="tpu_custom_call" | custom-call | tf_op jit(solution)/shard_map/pallas_call | solution.py:1031
  173.7 120.4 %shard_map.310 = (bf16[288,1280]{1,0:T(8,128)(2,1)}, f32[288,1280]{1,0:T(8,128)}, f32[144,1152]{1,0:T(8,128)}, f32[144,1152]{1,0:T(8,128)}, f32[3,144,288]{2,1,0...) custom-call(bf16[1280,1152]{1,0:T(8,128)(2,1)} %get-tuple-element.79, ...), custom_call_target="tpu_custom_call" | custom-call | tf_op jit(solution)/shard_map/pallas_call | solution.py:1781
  294.1 5.8 %shard_map.311 = (bf16[288,1280]{1,0:T(8,128)(2,1)}, f32[288,1280]{1,0:T(8,128)}, f32[144,1152]{1,0:T(8,128)}, f32[144,1152]{1,0:T(8,128)}, f32[3,144,288]{2,1,0...) custom-call(bf16[288,1280]{1,0:T(8,128)(2,1)} %get-tuple-element.103, ...), custom_call_target="tpu_custom_call" | custom-call | tf_op jit(solution)/shard_map/pallas_call | solution.py:1882
  299.9 0.8 slice.18
  300.7 0.1 reshape.56
  300.8 0.7 fusion.5
  301.5 0.7 slice.26
  302.1 0.1 slice.19
  302.2 0.6 slice.24
  (1 shorter events, 0.0 us)

commit v4 on v3

--- a/solution.py
+++ b/solution.py
@@ -1404,27 +1404,12 @@
         copy.start()
     for copy in fetches[:3]:
         copy.start()
-    greet(tok_at, mdl_at, tok_count, 4)
-    line = LineScatter(
-        tok_at, unit_grads, full_grads, unit_pieces, own_buf, own_sems, cross_in, passed, line_sends, line_recvs
-    )
-
-    mlps = ColumnReduce(
-        mdl_at, mlp_blocks, col_blocks.at[mdl_at], col_blocks.at[far_at], col_near, col_out, col_far, mlp_sends, mlp_recvs, size
-    )
-    ones = ColumnReduce(
-        mdl_at, col_blocks, col_blocks.at[mdl_at], col_blocks.at[far_at], col_near, col_out, col_far, one_sends, one_recvs, size
-    )
-    line.start(0, 4 * unit_pieces)
-    for chunk in range(chunks):
-        mlps.first(chunk)
     part_loads = [
         pltpu.make_async_copy(mlp_blocks.at[mdl_at], col_blocks.at[mdl_at], part_sems.at[0]),
         pltpu.make_async_copy(mlp_blocks.at[far_at], col_blocks.at[far_at], part_sems.at[1]),
     ]
     for copy in part_loads:
         copy.start()
-    line.load(0)
     for copy in fetches[3:]:
         copy.start()
     mod_load(0).start()
@@ -1436,6 +1421,21 @@
         key_flip[head] = k_heads[head].T
     for copy in part_loads:
         copy.wait()
+    greet(tok_at, mdl_at, tok_count, 4)
+    line = LineScatter(
+        tok_at, unit_grads, full_grads, unit_pieces, own_buf, own_sems, cross_in, passed, line_sends, line_recvs
+    )
+
+    mlps = ColumnReduce(
+        mdl_at, mlp_blocks, col_blocks.at[mdl_at], col_blocks.at[far_at], col_near, col_out, col_far, mlp_sends, mlp_recvs, size
+    )
+    ones = ColumnReduce(
+        mdl_at, col_blocks, col_blocks.at[mdl_at], col_blocks.at[far_at], col_near, col_out, col_far, one_sends, one_recvs, size
+    )
+    line.start(0, 4 * unit_pieces)
+    for chunk in range(chunks):
+        mlps.first(chunk)
+    line.load(0)
 
     def back_step(chunk, carry):
         slot = lax.rem(chunk, 2)

time: 304 us -> 308 us (1.013)
  Pallas kernels: 294 us -> 298 us
    pallas_call x1, Pallas kernels: 120 us -> 125 us  [rear(): pl.pallas_call(rear_kernel, out_shape=(shape((local_width, rows), bf16),...]
where the time goes in v4:
time: 308 us; the launch traced here: 307 us
  Pallas kernels  298 us (97%)
  local copies, waits for them, and re-layouts  4.44 us (1%)
  other arithmetic  3.39 us (1%)
    pallas_call x1, Pallas kernels, rear(): pl.pallas_call(rear_kernel, out_shape=(shape((local_width, rows), bf16),...  125 us
    pallas_call x1, Pallas kernels, front(): pl.pallas_call(front_kernel, out_shape=(shape((tok_count, slots, small_wi...  118 us
    pallas_call x1, Pallas kernels, feed(): pl.pallas_call(feed_kernel, out_shape=(jax.ShapeDtypeStruct((4, rows, loc...  50 us

profile of v4, /device:TPU:0, one launch (start us, length us, event | category | flops | bytes accessed | tf_op | source)
XLA Modules:
  0.0 307.0 jit_solution(8681967760047725507)
XLA Ops:
  0.6 0.7 convert_bitcast_fusion
  1.3 0.8 copy.35
  2.1 0.8 copy.36
  2.9 0.7 pad_add_fusion.masks
  3.5 0.7 fusion.4
  4.2 0.6 bitcast_convert_fusion.bias_table
  4.9 0.1 multiply_cosine_fusion
  5.0 0.6 select_maximum_fusion.feats_own
  5.6 118.1 %shard_map.308 = (f32[8,8,640]{2,1,0:T(8,128)}, f32[64,288]{1,0:T(8,128)}, bf16[64,144]{1,0:T(8,128)(2,1)}, f32[1,1152]{1,0:T(1,128)}, bf16[6,32,1152]{2,1,0:T(8...) custom-call(f32[8,256]{1,0:T(8,128)} %select_maximum_fusion.feats_ow, ...), custom_call_target="tpu_custom_call" | custom-call | tf_op jit(solution)/shard_map/pallas_call | solution.py:778
  123.7 50.0 %shard_map.309 = (bf16[4,1280,288]{2,1,0:T(8,128)(2,1)}, bf16[1280,1152]{1,0:T(8,128)(2,1)}, bf16[1152,2304]{1,0:T(8,128)(2,1)}, f32[1,1152]{1,0:T(1,128)}, f32[1,1152]{1,0:T(1,128)}) custom-call(bf16[1280,1152]{1,0:T(8,128)(2,1)} %get-tuple-element.69.branch_any.branch_full, bf16[1280,1152]{1,0:T(8,128)(2,1)} %get-tuple-element.70.tokens_full, ...), custom_call_target="tpu_custom_call" | custom-call | tf_op jit(solution)/shard_map/pallas_call | solution.py:1031
  173.7 124.5 %shard_map.310 = (bf16[288,1280]{1,0:T(8,128)(2,1)}, f32[288,1280]{1,0:T(8,128)}, f32[144,1152]{1,0:T(8,128)}, f32[144,1152]{1,0:T(8,128)}, f32[3,144,288]{2,1,0...) custom-call(bf16[1280,1152]{1,0:T(8,128)(2,1)} %get-tuple-element.79, ...), custom_call_target="tpu_custom_call" | custom-call | tf_op jit(solution)/shard_map/pallas_call | solution.py:1781
  298.2 5.8 %shard_map.311 = (bf16[288,1280]{1,0:T(8,128)(2,1)}, f32[288,1280]{1,0:T(8,128)}, f32[144,1152]{1,0:T(8,128)}, f32[144,1152]{1,0:T(8,128)}, f32[3,144,288]{2,1,0...) custom-call(bf16[288,1280]{1,0:T(8,128)(2,1)} %get-tuple-element.103, ...), custom_call_target="tpu_custom_call" | custom-call | tf_op jit(solution)/shard_map/pallas_call | solution.py:1882
  304.1 0.8 slice.18
  304.9 0.1 reshape.56
  305.0 0.7 fusion.5
  305.6 0.7 slice.26
  306.3 0.1 slice.19
  306.4 0.6 slice.24
  (1 shorter events, 0.0 us)
